TPU v7x, 32 devices: a whole 2x2x4 slice. The times are simulated.
32 devices in a mesh: lat: 8 (over z, core), lon: 4 (over y, x).
Axes of the slice: x: 2, y: 2, z: 4, core: 2. Of those that a mesh axis runs over, the one named last changes fastest.
Arguments:
- pedersen: float32 [16, 1024, 2048], P(None, 'lat', 'lon'), may hold values from 0.2 to 2
- hall_conductivity: float32 [16, 1024, 2048], P(None, 'lat', 'lon'), may hold values from 0.1 to 1.5
- east_wind: float32 [16, 1024, 2048], P(None, 'lat', 'lon'), may hold values from -6 to 6
- north_wind: float32 [16, 1024, 2048], P(None, 'lat', 'lon'), may hold values from -6 to 6
- ion_density: float32 [3, 1024, 2048], P(None, 'lat', 'lon'), may hold values from 0.5 to 2
Outputs:
- potential: float32 [1024, 2048], P('lat', 'lon')
- ion_update: float32 [3, 1024, 2048], P(None, 'lat', 'lon')
All inputs are finite; a program needn't handle non-finite values. Where the computation divides by a largest or mean magnitude, that divisor is 1e-20 or more.
Results may differ from a plain program's by a relative error of at most 0.00002.
Values sent between devices are 32-bit elements; how exact they have to be, the bound alone decides.
A program may use at most 192 MiB of HBM per device.

v0:
```python
import functools

import jax
import jax.numpy as jnp
from jax import lax
from jax.experimental import pallas as pl
from jax.experimental.pallas import tpu as pltpu
from jax.sharding import PartitionSpec as P

SWEEPS = 16
DAMPING = 0.0001
LOW_BOUND = 0.05
HIGH_BOUND = 2.0
COURANT = 0.8
MOBILITY = (1.0, 0.6, 0.3)
MESH = pl.DeviceIdType.MESH
GUARD = 24
HALO = 16
PIECES = 4
THETA = 0.5 * (HIGH_BOUND + LOW_BOUND)
F32 = jnp.float32
BF16 = jnp.bfloat16


def chebyshev_factors():
    delta = 0.5 * (HIGH_BOUND - LOW_BOUND)
    sigma_one = THETA / delta
    rho_prev = 1.0 / sigma_one
    first_list = []
    second_list = []
    for sweep in range(SWEEPS):
        rho_next = 1.0 / (2.0 * sigma_one - rho_prev)
        first_list.append(rho_next * rho_prev)
        second_list.append(2.0 * rho_next / delta)
        rho_prev = rho_next
    return first_list, second_list


def kernel(
    nlat, nlon, lev, rows, lt,
    ped_h, hall_h, east_h, north_h, ion_h,
    pot_o, upd_o,
    ped, hall, east, north,
    ion, ion_fr, ion_fl, ion_a, ion_b,
    sig, cur_e, cur_n, e_fr, e_fl, s_one, t_out, sig_rx, t_rx,
    S, src, s_fr, s_fl, v_fr, v_fl,
    lhs, to_strided, to_plain, coef,
    SP, U, SR, rR, mR, invR, spR, X, xr, xn, dnb,
    flux, mx, mrx,
    sem_in, sem_ion, ss, rs, ss_max, rs_max,
):
    n_rt = rows // 8
    nt = lt + 1
    width = nt * 128
    R = (rows + 2 * HALO) // 8
    n_dev = nlat * nlon
    me_lat = lax.axis_index("lat")
    me_lon = lax.axis_index("lon")
    has_up = me_lat > 0
    has_dn = me_lat < nlat - 1
    up = (jnp.maximum(me_lat - 1, 0), me_lon)
    dn = (jnp.minimum(me_lat + 1, nlat - 1), me_lon)
    lf = (me_lat, lax.rem(me_lon + nlon - 1, nlon))
    rt = (me_lat, lax.rem(me_lon + 1, nlon))
    mirror = (nlat - 1 - me_lat, me_lon)
    others = [
        (lax.rem(me_lat + a, nlat), lax.rem(me_lon + b, nlon))
        for a in range(nlat) for b in range(nlon) if a or b
    ]

    barrier = pltpu.get_barrier_semaphore()
    for dev in others:
        pl.semaphore_signal(barrier, inc=1, device_id=dev, device_id_type=MESH)

    per = n_rt // PIECES
    piece_order = [0, PIECES - 1] + list(range(1, PIECES - 1))
    hbm_in = (ped_h, hall_h, east_h, north_h)
    vm_in = (ped, hall, east, north)

    def in_copy(a, c):
        row = pl.multiple_of(8 * c, 8)
        return pltpu.make_async_copy(
            hbm_in[a].at[:, pl.ds(row, 8), :], vm_in[a].at[:, pl.ds(row, 8), :], sem_in.at[c, a]
        )

    def ion_copy(s, t):
        return pltpu.make_async_copy(
            ion_h.at[s, :, t * 128 : (t + 1) * 128], ion.at[s, t, 8 : 8 + rows], sem_ion.at[s, t]
        )

    for q in piece_order:
        for c in range(q * per, (q + 1) * per):
            for a in range(4):
                in_copy(a, c).start()
    for s in range(3):
        for t in range(lt):
            ion_copy(s, t).start()

    first_list, second_list = chebyshev_factors()
    for k in range(SWEEPS):
        coef[0, k] = jnp.float32(first_list[k])
        coef[1, k] = jnp.float32(second_list[k])

    counter = [0]

    def rcopy(src_ref, dst_ref, dev):
        k = counter[0]
        counter[0] += 1
        return pltpu.make_async_remote_copy(
            src_ref=src_ref, dst_ref=dst_ref, send_sem=ss.at[k], recv_sem=rs.at[k],
            device_id=dev, device_id_type=MESH,
        )

    lane = lax.broadcasted_iota(jnp.int32, (8, 128), 1)
    sub = lax.broadcasted_iota(jnp.int32, (8, 128), 0)

    def shifts(v):
        m = len(v)
        a = [pltpu.roll(t, 1, 1) for t in v]
        b = [pltpu.roll(t, 127, 1) for t in v]
        left = [jnp.where(lane == 0, a[j - 1], a[j]) for j in range(m)]
        right = [jnp.where(lane == 127, b[(j + 1) % m], b[j]) for j in range(m)]
        return left, right

    def rev8(v):
        v = pltpu.roll(v, 4, 0)
        for b in (2, 1):
            v = jnp.where((sub & b) == 0, pltpu.roll(v, 8 - b, 0), pltpu.roll(v, b, 0))
        return v

    @pl.loop(0, width // 16, unroll=4)
    def _(c):
        row = lax.broadcasted_iota(jnp.int32, (16, 128), 0) + 16 * c
        col = lax.broadcasted_iota(jnp.int32, (16, 128), 1)
        for t in range(nt):
            there = jnp.where(row == col * nt + t, 1.0, 0.0).astype(BF16)
            for part in range(3):
                at = pl.ds(pl.multiple_of(part * width + 16 * c, 16), 16)
                to_strided[at, t * 128 : (t + 1) * 128] = there

    weight = [(0.5 + l / lev) / lev for l in range(lev)]

    def columns(lo, hi):
        @pl.loop(lo, hi)
        def _(c):
            row = pl.multiple_of(8 * c, 8)
            for a in range(4):
                in_copy(a, c).wait()
            for t in range(lt):
                at = (pl.ds(row, 8), slice(t * 128, (t + 1) * 128))
                acc = [jnp.zeros((8, 128), F32)] * 3
                for l in range(lev):
                    p, h = weight[l] * ped[(l,) + at], weight[l] * hall[(l,) + at]
                    e, n = east[(l,) + at], north[(l,) + at]
                    acc = [acc[0] + p, acc[1] + (p * e + h * n), acc[2] + (p * n - h * e)]
                sig[t, pl.ds(row, 8), :] = acc[0]
                cur_e[t, pl.ds(row, 8), :] = acc[1]
                cur_n[t, pl.ds(row + 8, 8), :] = acc[2]

    sig_copies, e_copies = {}, {}
    n_up = rcopy(cur_n.at[:, 8:16], cur_n.at[:, rows + 8 : rows + 16], up)
    n_dn = rcopy(cur_n.at[:, rows : rows + 8], cur_n.at[:, 0:8], dn)
    i_up = rcopy(ion.at[:, :, 8:16], ion.at[:, :, rows + 8 : rows + 16], up)
    i_dn = rcopy(ion.at[:, :, rows : rows + 8], ion.at[:, :, 0:8], dn)
    i_lf = rcopy(ion.at[:, 0, 8 : 8 + rows], ion_fr, lf)
    i_rt = rcopy(ion.at[:, lt - 1, 8 : 8 + rows], ion_fl, rt)

    for i, q in enumerate(piece_order):
        columns(q * per, (q + 1) * per)
        if i == 0:
            pl.semaphore_wait(barrier, n_dev - 1)
        band = slice(q * per * 8, (q + 1) * per * 8)
        sig_copies[q] = rcopy(sig.at[:, band], sig_rx.at[:, band], mirror)
        sig_copies[q].start()
        if q == 0:
            @pl.when(has_up)
            def _():
                n_up.start()
        if q == PIECES - 1:
            @pl.when(has_dn)
            def _():
                n_dn.start()
        e_copies[q] = (
            rcopy(cur_e.at[0, band], e_fr.at[band], lf),
            rcopy(cur_e.at[lt - 1, band], e_fl.at[band], rt),
        )
        for c in e_copies[q]:
            c.start()

    for s in range(3):
        for t in range(lt):
            ion_copy(s, t).wait()

    @pl.when(has_up)
    def _():
        i_up.start()

    @pl.when(has_dn)
    def _():
        i_dn.start()

    i_lf.start()
    i_rt.start()

    @pl.when(jnp.logical_not(has_up))
    def _():
        cur_n[:, 0:8, :] = jnp.zeros((lt, 8, 128), F32)
        ion[:, :, 0:8, :] = jnp.zeros((3, lt, 8, 128), F32)
        S[:, 0:GUARD, :] = jnp.zeros((nt, GUARD, 128), F32)
        src[:, 0:GUARD, :] = jnp.zeros((nt, GUARD, 128), F32)

    @pl.when(jnp.logical_not(has_dn))
    def _():
        cur_n[:, rows + 8 : rows + 16, :] = jnp.zeros((lt, 8, 128), F32)
        ion[:, :, rows + 8 : rows + 16, :] = jnp.zeros((3, lt, 8, 128), F32)
        S[:, GUARD + rows :, :] = jnp.zeros((nt, GUARD, 128), F32)
        src[:, GUARD + rows :, :] = jnp.zeros((nt, GUARD, 128), F32)

    @pl.when(has_dn)
    def _():
        n_up.wait_recv()

    @pl.when(has_up)
    def _():
        n_dn.wait_recv()

    t_copies = {}
    for q in piece_order:
        for c in e_copies[q]:
            c.wait_recv()

        @pl.loop(q * per, (q + 1) * per, unroll=per)
        def _(c):
            row = pl.multiple_of(8 * c, 8)
            at = pl.ds(row, 8)
            tiles = [cur_e[t, at, :] for t in range(lt)]
            tiles.append(jnp.where(lane < 64, e_fr[at, :], e_fl[at, :]))
            left, right = shifts(tiles)
            for t in range(lt):
                d_lon = 0.5 * (right[t] - left[t])
                d_lat = 0.5 * (cur_n[t, pl.ds(row + 9, 8), :] - cur_n[t, pl.ds(row + 7, 8), :])
                s_one[t, at, :] = d_lon + d_lat
                t_out[t, at, :] = d_lon - d_lat

        band = slice(q * per * 8, (q + 1) * per * 8)
        t_copies[q] = rcopy(t_out.at[:, band], t_rx.at[:, band], mirror)
        t_copies[q].start()

    for j in range(nt):
        @pl.loop(0, 8, unroll=2)
        def _(c):
            row = lax.broadcasted_iota(jnp.int32, (16, 128), 0) + 16 * c
            col = lax.broadcasted_iota(jnp.int32, (16, 128), 1)
            home = row * nt + j
            for t in range(lt):
                here = col + t * 128
                back = jnp.where(home == here, 1.0, 0.0).astype(BF16)
                before = jnp.where(here == 0, width - 1, here - 1)
                slope = jnp.where(
                    home == here + 1, 0.5, jnp.where(home == before, -0.5, 0.0)
                ).astype(BF16)
                for part in range(3):
                    at = pl.ds(pl.multiple_of(part * width + j * 128 + 16 * c, 16), 16)
                    to_plain[at, t * 128 : (t + 1) * 128] = back
                    to_plain[at, (lt + t) * 128 : (lt + t + 1) * 128] = slope

    i_lf.wait_recv()
    i_rt.wait_recv()
    for s in range(3):
        @pl.loop(0, n_rt, unroll=4)
        def _(c):
            row = pl.multiple_of(8 * c, 8)
            at = pl.ds(row, 8)
            tiles = [ion[s, t, pl.ds(row + 8, 8), :] for t in range(lt)]
            tiles.append(jnp.where(lane < 64, ion_fr[s, at, :], ion_fl[s, at, :]))
            left, right = shifts(tiles)
            for t in range(lt):
                ion_a[s, t, at, :] = tiles[t] - left[t]
                ion_b[s, t, at, :] = right[t] - tiles[t]

    def combine(own, rx, out, q):
        @pl.loop((PIECES - 1 - q) * per, (PIECES - q) * per, unroll=per)
        def _(c):
            row = pl.multiple_of(8 * c, 8)
            back = pl.multiple_of(rows - 8 - 8 * c, 8)
            for t in range(lt):
                out[t, pl.ds(row + GUARD, 8), :] = own[t, pl.ds(row, 8), :] + rev8(
                    rx[t, pl.ds(back, 8), :]
                )

    def exchange(own, rx, copies, out, fr, fl, depth):
        lo_in, hi_in = slice(GUARD, GUARD + depth), slice(GUARD + rows - depth, GUARD + rows)
        lo_out, hi_out = slice(GUARD - depth, GUARD), slice(GUARD + rows, GUARD + rows + depth)
        c_up = rcopy(out.at[0:lt, lo_in], out.at[0:lt, hi_out], up)
        c_dn = rcopy(out.at[0:lt, hi_in], out.at[0:lt, lo_out], dn)
        lons = []

        def send_lon(part):
            lons.append(rcopy(out.at[0, part], fr.at[part], lf))
            lons.append(rcopy(out.at[lt - 1, part], fl.at[part], rt))
            lons[-2].start()
            lons[-1].start()

        def first(i):
            q = piece_order[i]
            copies[q].wait_recv()
            combine(own, rx, out, q)
            lo = GUARD + (PIECES - 1 - q) * per * 8
            if q == PIECES - 1:
                @pl.when(has_up)
                def _():
                    c_up.start()
            if q == 0:
                @pl.when(has_dn)
                def _():
                    c_dn.start()
            send_lon(slice(lo, lo + per * 8))

        def edges():
            @pl.when(has_up)
            def _():
                c_dn.wait_recv()

            send_lon(lo_out)

            @pl.when(has_dn)
            def _():
                c_up.wait_recv()

            send_lon(hi_out)

        first(0)
        first(1)
        for i in range(2, PIECES):
            first(i)
            if i == 2:
                edges()
        for c in lons:
            c.wait_recv()

        @pl.loop((GUARD - depth) // 8, (GUARD + rows + depth) // 8, unroll=4)
        def _(c):
            at = pl.ds(pl.multiple_of(8 * c, 8), 8)
            out[lt, at, :] = jnp.where(lane < 64, fr[at, :], fl[at, :])

        return c_up, c_dn, lons

    def split(v, at, t):
        for part in range(3):
            low = v.astype(BF16)
            lhs[at, part * width + t * 128 : part * width + (t + 1) * 128] = low
            v = v - low.astype(F32)

    def split_rows(ref, first, count):
        @pl.loop(0, count // 16, unroll=2)
        def _(c):
            row = pl.multiple_of(16 * c, 16)
            for t in range(nt):
                split(ref[t, pl.ds(pl.multiple_of(row + first, 8), 16), :], pl.ds(row, 16), t)

    def conv_lon(v):
        after = v[1:] + [pltpu.roll(v[0], 127, 1)]
        p = [a + b for a, b in zip(v, after)]
        before = [pltpu.roll(p[-1], 1, 1)] + p[:-1]
        return [a + b for a, b in zip(p, before)]

    s_up, s_dn, s_lons = exchange(sig, sig_rx, sig_copies, S, s_fr, s_fl, GUARD)
    tall = rows + 2 * GUARD
    ext = rows + 2 * HALO
    split_rows(S, 0, tall)
    moved = jnp.dot(lhs[0:tall, :], to_strided[...], preferred_element_type=F32)
    for t in range(nt):
        SP[t, :, :] = moved[:, t * 128 : (t + 1) * 128]

    @pl.loop(0, tall // 8, unroll=2)
    def _(c):
        at = pl.ds(pl.multiple_of(8 * c, 8), 8)
        for t, v in enumerate(conv_lon([SP[t, at, :] for t in range(nt)])):
            U[t, at, :] = v

    total = rows * nlat
    skip = GUARD - HALO
    for c in range(R):
        where = sub * R + (c - HALO + me_lat * rows)
        inside = (where >= 0) & (where < total)
        at = slice(8 * c, 8 * c + 8)
        for t in range(nt):
            s = SP[t, pl.ds(skip + c, 8, stride=R), :]
            around = U[t, pl.ds(skip + c - 1, 8, stride=R), :] + U[
                t, pl.ds(skip + c + 1, 8, stride=R), :
            ]
            around = around + 2.0 * U[t, pl.ds(skip + c, 8, stride=R), :]
            inv = jnp.where(inside, 1.0 / (DAMPING + 2.0 * s + 0.25 * around), 0.0)
            quarter = 0.25 * inv
            SR[t, at, :] = s
            invR[t, at, :] = inv
            rR[t, at, :] = quarter
            mR[t, at, :] = (THETA - 1.0) - 8.0 * (quarter * s)
            X[1, t, at, :] = jnp.zeros((8, 128), F32)

    v_up, v_dn, v_lons = exchange(s_one, t_rx, t_copies, src, v_fr, v_fl, HALO)
    split_rows(src, skip, ext)
    moved = jnp.dot(lhs[0:ext, :], to_strided[...], preferred_element_type=F32)
    for t in range(nt):
        SP[t, 0:ext, :] = moved[:, t * 128 : (t + 1) * 128]
    for c in range(R):
        at = slice(8 * c, 8 * c + 8)
        for t in range(nt):
            first = SP[t, pl.ds(c, 8, stride=R), :] * invR[t, at, :]
            spR[t, at, :] = first
            X[0, t, at, :] = first * (1.0 / THETA)

    def sweep(k, cur, prv, final):
        c1 = coef[0, k]
        c2 = coef[1, k]

        def smooth(c):
            at = slice(8 * c, 8 * c + 8)
            xs = [X[cur, t, at, :] for t in range(nt)]
            ys = [SR[t, at, :] * xs[t] for t in range(nt)]
            return xs, conv_lon(xs), conv_lon(ys)

        _, u_end, w_end = smooth(R - 1)
        xs, u, w = smooth(0)
        u_top, w_top = u, w
        qu = [pltpu.roll(a, 1, 0) + b for a, b in zip(u_end, u)]
        qw = [pltpu.roll(a, 1, 0) + b for a, b in zip(w_end, w)]
        for c in range(R):
            if c < R - 1:
                x_next, u_next, w_next = smooth(c + 1)
            else:
                x_next = None
                u_next = [pltpu.roll(v, 7, 0) for v in u_top]
                w_next = [pltpu.roll(v, 7, 0) for v in w_top]
            qu2 = [a + b for a, b in zip(u, u_next)]
            qw2 = [a + b for a, b in zip(w, w_next)]
            at = slice(8 * c, 8 * c + 8)
            for t in range(nt):
                pull = SR[t, at, :] * (qu[t] + qu2[t]) + (qw[t] + qw2[t])
                z = rR[t, at, :] * pull + (mR[t, at, :] * xs[t] + spR[t, at, :])
                new = c2 * z - c1 * X[prv, t, at, :]
                if final:
                    xr[t, pl.ds(8 + c, 8, stride=R), :] = new
                else:
                    X[prv, t, at, :] = new
            qu, qw, u, w, xs = qu2, qw2, u_next, w_next, x_next

    @pl.loop(0, (SWEEPS - 2) // 2)
    def _(k):
        sweep(2 * k, 0, 1, False)
        sweep(2 * k + 1, 1, 0, False)

    sweep(SWEEPS - 2, 0, 1, True)

    own0 = 8 + HALO
    best = jnp.zeros((8, 128), F32)
    for c in range(n_rt):
        lo = own0 + 8 * c
        x = [xr[t, lo : lo + 8, :] for t in range(nt)]
        after = x[1:] + [pltpu.roll(x[0], 127, 1)]
        before = [pltpu.roll(x[-1], 1, 1)] + x[:-1]
        for t in range(nt):
            speed = jnp.abs(0.5 * (xr[t, lo + 1 : lo + 9, :] - xr[t, lo - 1 : lo + 7, :]))
            speed = speed + jnp.abs(0.5 * (after[t] - before[t]))
            best = jnp.maximum(best, jnp.where(lane * nt + t < lt * 128, speed, 0.0))
    mx[0:1, :] = jnp.max(best, axis=0, keepdims=True)

    max_copies = []
    for o, dev in enumerate(others):
        max_copies.append(
            pltpu.make_async_remote_copy(
                src_ref=mx.at[0:1], dst_ref=mrx.at[o : o + 1],
                send_sem=ss_max.at[o], recv_sem=rs_max.at[o],
                device_id=dev, device_id_type=MESH,
            )
        )
        max_copies[-1].start()

    near = rows + 16
    split_rows(xr, own0 - 8, near)
    moved = jnp.dot(lhs[0:near, :], to_plain[...], preferred_element_type=F32)
    for t in range(lt):
        xn[t, :, :] = moved[:, t * 128 : (t + 1) * 128]
        dnb[t, :, :] = moved[:, (lt + t) * 128 : (lt + t + 1) * 128]
        pot_o[:, t * 128 : (t + 1) * 128] = moved[8 : 8 + rows, t * 128 : (t + 1) * 128]

    @pl.when(has_dn)
    def _():
        i_up.wait_recv()

    @pl.when(has_up)
    def _():
        i_dn.wait_recv()

    @pl.loop(0, n_rt, unroll=2)
    def _(c):
        row = pl.multiple_of(8 * c, 8)
        at = pl.ds(row, 8)
        for t in range(lt):
            de = -0.5 * (xn[t, pl.ds(row + 9, 8), :] - xn[t, pl.ds(row + 7, 8), :])
            dv = dnb[t, pl.ds(row + 8, 8), :]
            e_pos, e_neg = jnp.maximum(de, 0.0), jnp.minimum(de, 0.0)
            n_pos, n_neg = jnp.maximum(dv, 0.0), jnp.minimum(dv, 0.0)
            for s in range(3):
                n = ion[s, t, pl.ds(row + 8, 8), :]
                f = e_pos * ion_a[s, t, at, :] + e_neg * ion_b[s, t, at, :]
                f = f + n_pos * (n - ion[s, t, pl.ds(row + 7, 8), :])
                f = f + n_neg * (ion[s, t, pl.ds(row + 9, 8), :] - n)
                flux[s, t, at, :] = f

    for c in max_copies:
        c.wait_recv()
    best = jnp.maximum(
        jnp.max(mrx[0 : n_dev - 1, :], axis=0, keepdims=True), mx[0:1, :]
    )
    best = jnp.max(best, axis=1, keepdims=True)
    step = jnp.broadcast_to(COURANT / (best + 1e-6), (8, 128))

    for s in range(3):
        scale = MOBILITY[s] * step

        @pl.loop(0, n_rt, unroll=2)
        def _(c):
            row = pl.multiple_of(8 * c, 8)
            for t in range(lt):
                upd_o[s, pl.ds(row, 8), t * 128 : (t + 1) * 128] = (
                    ion[s, t, pl.ds(row + 8, 8), :] - scale * flux[s, t, pl.ds(row, 8), :]
                )

    @pl.when(has_up)
    def _():
        for c in (n_up, i_up, s_up, v_up):
            c.wait_send()

    @pl.when(has_dn)
    def _():
        for c in (n_dn, i_dn, s_dn, v_dn):
            c.wait_send()

    done = [i_lf, i_rt] + s_lons + v_lons + max_copies
    for q in piece_order:
        done += [sig_copies[q], t_copies[q]] + list(e_copies[q])
    for c in done:
        c.wait_send()


def solution(mesh):
    nlat, nlon = mesh.shape["lat"], mesh.shape["lon"]

    def shards(pedersen, hall_conductivity, east_wind, north_wind, ion_density):
        lev, rows, cols = pedersen.shape
        lt = cols // 128
        nt = lt + 1
        width = nt * 128
        tall = rows + 2 * GUARD
        ext = rows + 2 * HALO
        others = nlat * nlon - 1
        vm = lambda *shape: pltpu.VMEM(shape, F32)
        half = lambda *shape: pltpu.VMEM(shape, BF16)
        dma = lambda *shape: pltpu.SemaphoreType.DMA(shape)
        hbm = pl.BlockSpec(memory_space=pltpu.HBM)
        return pl.pallas_call(
            functools.partial(kernel, nlat, nlon, lev, rows, lt),
            out_shape=(pltpu.VMEM((rows, cols), F32), pltpu.VMEM((3, rows, cols), F32)),
            in_specs=[hbm] * 5,
            out_specs=(pl.BlockSpec(memory_space=pltpu.VMEM),) * 2,
            scratch_shapes=[vm(lev, rows, cols)] * 4
            + [vm(3, lt, rows + 16, 128)] + [vm(3, rows, 128)] * 2 + [vm(3, lt, rows, 128)] * 2
            + [vm(lt, rows, 128), vm(lt, rows, 128), vm(lt, rows + 16, 128)]
            + [vm(rows, 128)] * 2
            + [vm(lt, rows, 128)] * 4
            + [vm(nt, tall, 128)] * 2 + [vm(tall, 128)] * 4
            + [half(tall, 3 * width), half(3 * width, width), half(3 * width, 2 * lt * 128)]
            + [pltpu.SMEM((2, SWEEPS), F32)]
            + [vm(nt, tall, 128)] * 2
            + [vm(nt, ext, 128)] * 5
            + [vm(2, nt, ext, 128), vm(nt, ext + 16, 128)]
            + [vm(lt, rows + 16, 128)] * 2
            + [vm(3, lt, rows, 128), vm(8, 128), vm(others + 1, 128)]
            + [dma(rows // 8, 4), dma(3, lt), dma(54), dma(54), dma(others), dma(others)],
            compiler_params=pltpu.CompilerParams(
                collective_id=0, has_side_effects=True, vmem_limit_bytes=60 * 1024 * 1024
            ),
        )(pedersen, hall_conductivity, east_wind, north_wind, ion_density)

    spec = P(None, "lat", "lon")
    return jax.shard_map(
        shards,
        mesh=mesh,
        in_specs=(spec,) * 5,
        out_specs=(P("lat", "lon"), spec),
        check_vma=False,
    )
```

profile of v0, /device:TPU:0, one launch (start us, length us, event | category | flops | bytes accessed | tf_op | source)
XLA Modules:
  0.0 58.5 jit_solution(18201506742690083399)
XLA Ops:
  0.6 56.3 %shard_map.68 = (f32[128,512]{1,0:T(8,128)S(1)}, f32[3,128,512]{2,1,0:T(8,128)S(1)}) custom-call(f32[16,128,512]{2,1,0:T(8,128)} %ped_h.1, f32[16,128,512]{2,1,0:T(8,128)} %hall_h.1, f32[16,128,512]{2,1,0:T(8,128)} %east_h.1, f32[16,128,512]{2,1,0:T(8,128)} %north_h.1, f32[3,128,512]{2,1,0:T(8,128)} %ion_h.1), custom_call_target="tpu_custom_call" | custom-call | tf_op jit(solution)/shard_map/pallas_call | solution.py:562
  56.9 0.7 %copy.9 = f32[128,512]{1,0:T(8,128)} copy(f32[128,512]{1,0:T(8,128)S(1)} %get-tuple-element.2) | data formatting | bytes 524288
  57.6 0.9 %copy.10 = f32[3,128,512]{2,1,0:T(8,128)} copy(f32[3,128,512]{2,1,0:T(8,128)S(1)} %get-tuple-element.3) | data formatting | bytes 1572864
where the time goes:
time: 58.7 us; the launch traced here: 58.5 us
  Pallas kernels  56.3 us (96%)
  local copies, waits for them, and re-layouts  1.58 us (3%)
  between operations  0.64 us (1%)
    pallas_call x1, Pallas kernels, shards(): pl.pallas_call(functools.partial(kernel, nlat, nlon, lev, rows, lt), out_...  56.3 us
    unnamed x2, local copies, waits for them, and re-layouts  1.58 us

commit v1 on v0

v1 whole, which is shorter than its diff:
```python
import functools

import jax
import jax.numpy as jnp
from jax import lax
from jax.experimental import pallas as pl
from jax.experimental.pallas import tpu as pltpu
from jax.sharding import PartitionSpec as P

SWEEPS = 16
DAMPING = 0.0001
LOW_BOUND = 0.05
HIGH_BOUND = 2.0
COURANT = 0.8
MOBILITY = (1.0, 0.6, 0.3)
MESH = pl.DeviceIdType.MESH
GUARD = 24
HALO = 16
PIECES = 4
THETA = 0.5 * (HIGH_BOUND + LOW_BOUND)
F32 = jnp.float32
BF16 = jnp.bfloat16


def chebyshev_factors():
    delta = 0.5 * (HIGH_BOUND - LOW_BOUND)
    sigma_one = THETA / delta
    rho_prev = 1.0 / sigma_one
    first_list = []
    second_list = []
    for sweep in range(SWEEPS):
        rho_next = 1.0 / (2.0 * sigma_one - rho_prev)
        first_list.append(rho_next * rho_prev)
        second_list.append(2.0 * rho_next / delta)
        rho_prev = rho_next
    return first_list, second_list


RECV = ("e", "ion", "n_up", "n_dn", "i_up", "i_dn", "sig_a", "sig_b", "t_a", "t_b", "t_c",
        "s_up", "s_dn", "s_lon", "v_up", "v_dn", "v_lon", "v_last", "max")
SEND = ("sig", "t", "lon", "up", "dn", "max")
EDGE = 32


def in_groups(n_rt):
    per = n_rt // PIECES
    spans = [(0, 1), (n_rt - 1, n_rt), (1, per), (n_rt - per, n_rt - 1)]
    for q in range(1, PIECES - 1):
        half = q * per + per // 2
        spans += [(q * per, half), (half, (q + 1) * per)]
    return [p for p in spans if p[1] > p[0]]


def kernel(
    nlat, nlon, lev, rows, lt,
    ped_h, hall_h, east_h, north_h, ion_h,
    pot_o, upd_o,
    vin, ion, ion_a, ion_b,
    sig, cur_e, cur_n, s_one, t_out, sig_rx, t_rx,
    S, src, pk, rx_e, rx_ion, rx_s, rx_v,
    lhs, to_strided, to_plain, coef,
    SP, U, SR, rR, mR, invR, spR, X, xr, xn, dnb,
    flux, mx, mrx,
    sem_in, sem_ion, ss, rs,
):
    n_rt = rows // 8
    nt = lt + 1
    width = nt * 128
    R = (rows + 2 * HALO) // 8
    n_dev = nlat * nlon
    me_lat = lax.axis_index("lat")
    me_lon = lax.axis_index("lon")
    has_up = me_lat > 0
    has_dn = me_lat < nlat - 1
    up = (jnp.maximum(me_lat - 1, 0), me_lon)
    dn = (jnp.minimum(me_lat + 1, nlat - 1), me_lon)
    lf = (me_lat, lax.rem(me_lon + nlon - 1, nlon))
    rt = (me_lat, lax.rem(me_lon + 1, nlon))
    mirror = (nlat - 1 - me_lat, me_lon)
    others = [
        (lax.rem(me_lat + a, nlat), lax.rem(me_lon + b, nlon))
        for a in range(nlat) for b in range(nlon) if a or b
    ]

    barrier = pltpu.get_barrier_semaphore()
    for dev in others:
        pl.semaphore_signal(barrier, inc=1, device_id=dev, device_id_type=MESH)

    per = n_rt // PIECES
    groups = in_groups(n_rt)

    def in_copy(a, g):
        at = slice(8 * groups[g][0], 8 * groups[g][1])
        return pltpu.make_async_copy(
            (ped_h, hall_h, east_h, north_h)[a].at[:, at, :], vin.at[a, :, at, :], sem_in.at[g]
        )

    for g in range(len(groups)):
        for a in range(4):
            in_copy(a, g).start()
    for s in range(3):
        for t in range(lt):
            pltpu.make_async_copy(
                ion_h.at[s, :, t * 128 : (t + 1) * 128], ion.at[s, t, 8 : 8 + rows], sem_ion.at[0]
            ).start()

    first_list, second_list = chebyshev_factors()
    for k in range(SWEEPS):
        coef[0, k] = jnp.float32(first_list[k])
        coef[1, k] = jnp.float32(second_list[k])

    def rcopy(src_ref, dst_ref, dev, send, recv):
        return pltpu.make_async_remote_copy(
            src_ref=src_ref, dst_ref=dst_ref,
            send_sem=ss.at[SEND.index(send)], recv_sem=rs.at[RECV.index(recv)],
            device_id=dev, device_id_type=MESH,
        )

    def arrived(name, view):
        pltpu.make_async_copy(view, view, rs.at[RECV.index(name)]).wait()

    def sent(name, view):
        pltpu.make_async_copy(view, view, ss.at[SEND.index(name)]).wait()

    lane = lax.broadcasted_iota(jnp.int32, (8, 128), 1)
    sub = lax.broadcasted_iota(jnp.int32, (8, 128), 0)

    def turn(v, by):
        by = by % 128
        return pltpu.roll(v, by, 1) if by else v

    def shifts(v, after, before):
        a = [pltpu.roll(t, 1, 1) for t in v]
        b = [pltpu.roll(t, 127, 1) for t in v] + [after]
        left = [jnp.where(lane == 0, p, q) for p, q in zip([before] + a[:-1], a)]
        right = [jnp.where(lane == 127, p, q) for p, q in zip(b[1:], b[:-1])]
        return left, right

    def pack(slot, tiles, step, skip):
        acc = None
        for k, v in enumerate(tiles):
            v = turn(v, step * k + skip)
            acc = v if k == 0 else jnp.where(lane < step * k, acc, v)
        pk[slot, :, :] = acc

    def rev8(v):
        v = pltpu.roll(v, 4, 0)
        for b in (2, 1):
            v = jnp.where((sub & b) == 0, pltpu.roll(v, 8 - b, 0), pltpu.roll(v, b, 0))
        return v

    @pl.loop(0, width // 16, unroll=4)
    def _(c):
        row = lax.broadcasted_iota(jnp.int32, (16, 128), 0) + 16 * c
        col = lax.broadcasted_iota(jnp.int32, (16, 128), 1)
        for t in range(nt):
            there = jnp.where(row == col * nt + t, 1.0, 0.0).astype(BF16)
            for part in range(3):
                at = pl.ds(pl.multiple_of(part * width + 16 * c, 16), 16)
                to_strided[at, t * 128 : (t + 1) * 128] = there

    weight = [(0.5 + l / lev) / lev for l in range(lev)]

    def columns(g):
        lo, hi = groups[g]
        view = vin.at[:, :, 8 * lo : 8 * hi, :]
        pltpu.make_async_copy(view, view, sem_in.at[g]).wait()

        @pl.loop(lo, hi)
        def _(c):
            row = pl.multiple_of(8 * c, 8)
            for t in range(lt):
                at = (pl.ds(row, 8), slice(t * 128, (t + 1) * 128))
                acc = [jnp.zeros((8, 128), F32)] * 3
                for l in range(lev):
                    p, h = weight[l] * vin[(0, l) + at], weight[l] * vin[(1, l) + at]
                    e, n = vin[(2, l) + at], vin[(3, l) + at]
                    acc = [acc[0] + p, acc[1] + (p * e + h * n), acc[2] + (p * n - h * e)]
                sig[t, pl.ds(row, 8), :] = acc[0]
                cur_e[t, pl.ds(row, 8), :] = acc[1]
                cur_n[t, pl.ds(row + 8, 8), :] = acc[2]

    def band(q):
        return slice(q * per * 8, (q + 1) * per * 8)

    def send_sig(q, recv):
        rcopy(sig.at[:, band(q)], sig_rx.at[:, band(q)], mirror, "sig", recv).start()

    def send_t(q, recv):
        rcopy(t_out.at[:, band(q)], t_rx.at[:, band(q)], mirror, "t", recv).start()

    def to_up(src_ref, dst_ref, recv):
        @pl.when(has_up)
        def _():
            rcopy(src_ref, dst_ref, up, "up", recv).start()

    def to_dn(src_ref, dst_ref, recv):
        @pl.when(has_dn)
        def _():
            rcopy(src_ref, dst_ref, dn, "dn", recv).start()

    def from_dn(name, view):
        @pl.when(has_dn)
        def _():
            arrived(name, view)

    def from_up(name, view):
        @pl.when(has_up)
        def _():
            arrived(name, view)

    def send_lon(slot, rx, g, recv):
        rcopy(pk.at[slot], rx.at[0, g], lf, "lon", recv).start()
        rcopy(pk.at[slot + 1], rx.at[1, g], rt, "lon", recv).start()

    columns(0)
    columns(1)
    pl.semaphore_wait(barrier, n_dev - 1)
    to_up(cur_n.at[:, 8:16], cur_n.at[:, rows + 8 : rows + 16], "n_up")
    to_dn(cur_n.at[:, rows : rows + 8], cur_n.at[:, 0:8], "n_dn")
    columns(2)
    send_sig(0, "sig_a")
    columns(3)
    send_sig(PIECES - 1, "sig_a")
    for q in range(1, PIECES - 1):
        columns(2 * q + 2)
        columns(2 * q + 3)
        send_sig(q, "sig_b")

    step_e = 128 // n_rt
    pack(0, [cur_e[0, 8 * c : 8 * c + 8, :] for c in range(n_rt)], step_e, 0)
    pack(1, [cur_e[lt - 1, 8 * c : 8 * c + 8, :] for c in range(n_rt)], step_e, 1)
    send_lon(0, rx_e, 0, "e")

    @pl.when(jnp.logical_not(has_up))
    def _():
        cur_n[:, 0:8, :] = jnp.zeros((lt, 8, 128), F32)
        ion[:, :, 0:8, :] = jnp.zeros((3, lt, 8, 128), F32)
        S[:, 0:GUARD, :] = jnp.zeros((nt, GUARD, 128), F32)
        src[:, 0:GUARD, :] = jnp.zeros((nt, GUARD, 128), F32)

    @pl.when(jnp.logical_not(has_dn))
    def _():
        cur_n[:, rows + 8 : rows + 16, :] = jnp.zeros((lt, 8, 128), F32)
        ion[:, :, rows + 8 : rows + 16, :] = jnp.zeros((3, lt, 8, 128), F32)
        S[:, GUARD + rows :, :] = jnp.zeros((nt, GUARD, 128), F32)
        src[:, GUARD + rows :, :] = jnp.zeros((nt, GUARD, 128), F32)

    view = ion.at[:, :, 8 : 8 + rows]
    pltpu.make_async_copy(view, view, sem_ion.at[0]).wait()
    step_i = 128 // (3 * n_rt)
    bands = [(s, c) for s in range(3) for c in range(n_rt)]
    pack(2, [ion[s, 0, 8 * c + 8 : 8 * c + 16, :] for s, c in bands], step_i, 0)
    pack(3, [ion[s, lt - 1, 8 * c + 8 : 8 * c + 16, :] for s, c in bands], step_i, 1)
    send_lon(2, rx_ion, 0, "ion")

    from_dn("n_up", cur_n.at[:, 0:8])
    from_up("n_dn", cur_n.at[:, 0:8])
    arrived("e", rx_e)
    e_fr, e_fl = rx_e[0, 0, :, :], rx_e[1, 0, :, :]
    for q in [0, PIECES - 1] + list(range(1, PIECES - 1)):
        for c in range(q * per, (q + 1) * per):
            row = 8 * c
            at = slice(row, row + 8)
            left, right = shifts(
                [cur_e[t, at, :] for t in range(lt)],
                turn(e_fr, 127 - step_e * c), turn(e_fl, 128 - step_e * c),
            )
            for t in range(lt):
                d_lon = 0.5 * (right[t] - left[t])
                d_lat = 0.5 * (cur_n[t, row + 9 : row + 17, :] - cur_n[t, row + 7 : row + 15, :])
                s_one[t, at, :] = d_lon + d_lat
                t_out[t, at, :] = d_lon - d_lat
        if q in (0, PIECES - 1):
            send_t(q, "t_a")

    for j in range(nt):
        @pl.loop(0, 8, unroll=2)
        def _(c):
            row = lax.broadcasted_iota(jnp.int32, (16, 128), 0) + 16 * c
            col = lax.broadcasted_iota(jnp.int32, (16, 128), 1)
            home = row * nt + j
            for t in range(lt):
                here = col + t * 128
                back = jnp.where(home == here, 1.0, 0.0).astype(BF16)
                before = jnp.where(here == 0, width - 1, here - 1)
                slope = jnp.where(
                    home == here + 1, 0.5, jnp.where(home == before, -0.5, 0.0)
                ).astype(BF16)
                for part in range(3):
                    at = pl.ds(pl.multiple_of(part * width + j * 128 + 16 * c, 16), 16)
                    to_plain[at, t * 128 : (t + 1) * 128] = back
                    to_plain[at, (lt + t) * 128 : (lt + t + 1) * 128] = slope

    def combine(own, rx, out, q):
        p = PIECES - 1 - q
        for c in range(p * per, (p + 1) * per):
            back = rows - 8 - 8 * c
            for t in range(lt):
                out[t, 8 * c + GUARD : 8 * c + GUARD + 8, :] = own[
                    t, 8 * c : 8 * c + 8, :
                ] + rev8(rx[t, back : back + 8, :])

    def spread(out, rx, slot, g, lo, count, recv):
        tiles = lambda t: [out[t, lo + 8 * k : lo + 8 * k + 8, :] for k in range(count)]
        pack(slot, tiles(0), EDGE, 0)
        pack(slot + 1, tiles(lt - 1), EDGE, EDGE)
        send_lon(slot, rx, g, recv)

    def gather(out, rx, g, lo, count):
        fr, fl = rx[0, g, :, :], rx[1, g, :, :]
        for k in range(count):
            a, b = turn(fr, 128 - EDGE * k), turn(fl, 256 - EDGE - EDGE * k)
            out[lt, lo + 8 * k : lo + 8 * k + 8, :] = jnp.where(
                lane < EDGE, a, jnp.where(lane >= 128 - EDGE, b, 0.0)
            )

    def spread_piece(out, rx, slot, q, recv):
        p = PIECES - 1 - q
        spread(out, rx, slot + 2 * p, p, GUARD + p * per * 8, per, recv)

    def gather_piece(out, rx, q):
        p = PIECES - 1 - q
        gather(out, rx, p, GUARD + p * per * 8, per)

    def lat_send(out, depth, name):
        lo, hi = GUARD, GUARD + rows
        to_up(out.at[0:lt, lo : lo + depth], out.at[0:lt, hi : hi + depth], name + "_up")
        to_dn(out.at[0:lt, hi - depth : hi], out.at[0:lt, lo - depth : lo], name + "_dn")

    def lat_spread(out, rx, depth, name, slot):
        lo, hi = GUARD, GUARD + rows
        from_up(name + "_dn", out.at[0:lt, lo - depth : lo])
        spread(out, rx, slot + 2 * PIECES, PIECES, lo - depth, depth // 8, name + "_lon")
        from_dn(name + "_up", out.at[0:lt, lo - depth : lo])
        spread(out, rx, slot + 2 * PIECES + 2, PIECES + 1, hi, depth // 8, name + "_lon")

    def lat_gather(out, rx, depth):
        gather(out, rx, PIECES, GUARD - depth, depth // 8)
        gather(out, rx, PIECES + 1, GUARD + rows, depth // 8)

    outer, inner = [0, PIECES - 1], list(range(1, PIECES - 1))
    slot_s, slot_v = 4, 4 + 2 * (PIECES + 2)

    arrived("sig_a", sig_rx.at[:, 0 : 2 * per * 8])
    for q in outer:
        combine(sig, sig_rx, S, q)
    lat_send(S, GUARD, "s")
    for q in inner[:-1]:
        send_t(q, "t_b")
    for q in outer:
        spread_piece(S, rx_s, slot_s, q, "s_lon")
    arrived("sig_b", sig_rx.at[:, 0 : (PIECES - 2) * per * 8])
    for q in inner:
        combine(sig, sig_rx, S, q)
        spread_piece(S, rx_s, slot_s, q, "s_lon")

    arrived("ion", rx_ion)
    i_fr, i_fl = rx_ion[0, 0, :, :], rx_ion[1, 0, :, :]
    for k, (s, c) in enumerate(bands):
        at = slice(8 * c, 8 * c + 8)
        tiles = [ion[s, t, 8 * c + 8 : 8 * c + 16, :] for t in range(lt)]
        left, right = shifts(tiles, turn(i_fr, 127 - step_i * k), turn(i_fl, 128 - step_i * k))
        for t in range(lt):
            ion_a[s, t, at, :] = tiles[t] - left[t]
            ion_b[s, t, at, :] = right[t] - tiles[t]

    lat_spread(S, rx_s, GUARD, "s", slot_s)
    arrived("s_lon", rx_s)
    for q in outer + inner:
        gather_piece(S, rx_s, q)
    lat_gather(S, rx_s, GUARD)

    def split(v, at, t):
        for part in range(3):
            low = v.astype(BF16)
            lhs[at, part * width + t * 128 : part * width + (t + 1) * 128] = low
            v = v - low.astype(F32)

    def split_rows(ref, first, lo, hi):
        for row in range(lo, hi, 16):
            for t in range(nt):
                split(ref[t, row + first : row + first + 16, :], slice(row, row + 16), t)

    def conv_lon(v):
        after = v[1:] + [pltpu.roll(v[0], 127, 1)]
        p = [a + b for a, b in zip(v, after)]
        before = [pltpu.roll(p[-1], 1, 1)] + p[:-1]
        return [a + b for a, b in zip(p, before)]

    tall = rows + 2 * GUARD
    ext = rows + 2 * HALO
    split_rows(S, 0, 0, tall)
    moved = jnp.dot(lhs[0:tall, :], to_strided[...], preferred_element_type=F32)
    for t in range(nt):
        SP[t, :, :] = moved[:, t * 128 : (t + 1) * 128]

    for c in range(tall // 8):
        for t, v in enumerate(conv_lon([SP[t, 8 * c : 8 * c + 8, :] for t in range(nt)])):
            U[t, 8 * c : 8 * c + 8, :] = v

    total = rows * nlat
    skip = GUARD - HALO
    for c in range(R):
        where = sub * R + (c - HALO + me_lat * rows)
        inside = (where >= 0) & (where < total)
        at = slice(8 * c, 8 * c + 8)
        for t in range(nt):
            s = SP[t, pl.ds(skip + c, 8, stride=R), :]
            around = U[t, pl.ds(skip + c - 1, 8, stride=R), :] + U[
                t, pl.ds(skip + c + 1, 8, stride=R), :
            ]
            around = around + 2.0 * U[t, pl.ds(skip + c, 8, stride=R), :]
            inv = jnp.where(inside, 1.0 / (DAMPING + 2.0 * s + 0.25 * around), 0.0)
            quarter = 0.25 * inv
            SR[t, at, :] = s
            invR[t, at, :] = inv
            rR[t, at, :] = quarter
            mR[t, at, :] = (THETA - 1.0) - 8.0 * (quarter * s)
            X[1, t, at, :] = jnp.zeros((8, 128), F32)

    arrived("t_a", t_rx.at[:, 0 : 2 * per * 8])
    for q in outer:
        combine(s_one, t_rx, src, q)
    lat_send(src, HALO, "v")
    send_t(inner[-1], "t_c")
    to_up(ion.at[:, :, 8:16], ion.at[:, :, rows + 8 : rows + 16], "i_up")
    to_dn(ion.at[:, :, rows : rows + 8], ion.at[:, :, 0:8], "i_dn")
    for q in outer:
        spread_piece(src, rx_v, slot_v, q, "v_lon")
    arrived("t_b", t_rx.at[:, 0 : (PIECES - 3) * per * 8])
    for q in inner[:-1]:
        combine(s_one, t_rx, src, q)
        spread_piece(src, rx_v, slot_v, q, "v_lon")
    lat_spread(src, rx_v, HALO, "v", slot_v)
    arrived("v_lon", pk.at[0 : 2 * (PIECES + 1)])
    for q in outer + inner[:-1]:
        gather_piece(src, rx_v, q)
    lat_gather(src, rx_v, HALO)
    last = PIECES - 1 - inner[-1]
    last_lo, last_hi = HALO + last * per * 8, HALO + (last + 1) * per * 8
    for lo, hi in ((0, last_lo), (last_hi, ext)):
        split_rows(src, skip, lo, hi)
        moved = jnp.dot(lhs[lo:hi, :], to_strided[...], preferred_element_type=F32)
        for t in range(nt):
            SP[t, lo:hi, :] = moved[:, t * 128 : (t + 1) * 128]

    arrived("t_c", t_rx.at[:, 0 : per * 8])
    combine(s_one, t_rx, src, inner[-1])
    spread_piece(src, rx_v, slot_v, inner[-1], "v_last")
    arrived("v_last", pk.at[0:2])
    gather_piece(src, rx_v, inner[-1])
    split_rows(src, skip, last_lo, last_hi)
    moved = jnp.dot(lhs[last_lo:last_hi, :], to_strided[...], preferred_element_type=F32)
    for t in range(nt):
        SP[t, last_lo:last_hi, :] = moved[:, t * 128 : (t + 1) * 128]
    for c in range(R):
        at = slice(8 * c, 8 * c + 8)
        for t in range(nt):
            first = SP[t, pl.ds(c, 8, stride=R), :] * invR[t, at, :]
            spR[t, at, :] = first
            X[0, t, at, :] = first * (1.0 / THETA)

    def sweep(k, cur, prv, final):
        c1 = coef[0, k]
        c2 = coef[1, k]

        def smooth(c):
            at = slice(8 * c, 8 * c + 8)
            xs = [X[cur, t, at, :] for t in range(nt)]
            ys = [SR[t, at, :] * xs[t] for t in range(nt)]
            return xs, conv_lon(xs), conv_lon(ys)

        _, u_end, w_end = smooth(R - 1)
        xs, u, w = smooth(0)
        u_top, w_top = u, w
        qu = [pltpu.roll(a, 1, 0) + b for a, b in zip(u_end, u)]
        qw = [pltpu.roll(a, 1, 0) + b for a, b in zip(w_end, w)]
        for c in range(R):
            if c < R - 1:
                x_next, u_next, w_next = smooth(c + 1)
            else:
                x_next = None
                u_next = [pltpu.roll(v, 7, 0) for v in u_top]
                w_next = [pltpu.roll(v, 7, 0) for v in w_top]
            qu2 = [a + b for a, b in zip(u, u_next)]
            qw2 = [a + b for a, b in zip(w, w_next)]
            at = slice(8 * c, 8 * c + 8)
            for t in range(nt):
                pull = SR[t, at, :] * (qu[t] + qu2[t]) + (qw[t] + qw2[t])
                z = rR[t, at, :] * pull + (mR[t, at, :] * xs[t] + spR[t, at, :])
                new = c2 * z - c1 * X[prv, t, at, :]
                if final:
                    xr[t, pl.ds(8 + c, 8, stride=R), :] = new
                else:
                    X[prv, t, at, :] = new
            qu, qw, u, w, xs = qu2, qw2, u_next, w_next, x_next

    @pl.loop(0, (SWEEPS - 2) // 2)
    def _(k):
        sweep(2 * k, 0, 1, False)
        sweep(2 * k + 1, 1, 0, False)

    sweep(SWEEPS - 2, 0, 1, True)

    own0 = 8 + HALO
    best = jnp.zeros((8, 128), F32)
    for c in range(n_rt):
        lo = own0 + 8 * c
        x = [xr[t, lo : lo + 8, :] for t in range(nt)]
        after = x[1:] + [pltpu.roll(x[0], 127, 1)]
        before = [pltpu.roll(x[-1], 1, 1)] + x[:-1]
        for t in range(nt):
            speed = jnp.abs(0.5 * (xr[t, lo + 1 : lo + 9, :] - xr[t, lo - 1 : lo + 7, :]))
            speed = speed + jnp.abs(0.5 * (after[t] - before[t]))
            best = jnp.maximum(best, jnp.where(lane * nt + t < lt * 128, speed, 0.0))
    mx[0:1, :] = jnp.max(best, axis=0, keepdims=True)

    for o, dev in enumerate(others):
        rcopy(mx.at[0:1], mrx.at[o : o + 1], dev, "max", "max").start()

    near = rows + 16
    split_rows(xr, own0 - 8, 0, near)
    moved = jnp.dot(lhs[0:near, :], to_plain[...], preferred_element_type=F32)
    for t in range(lt):
        xn[t, :, :] = moved[:, t * 128 : (t + 1) * 128]
        dnb[t, :, :] = moved[:, (lt + t) * 128 : (lt + t + 1) * 128]
        pot_o[:, t * 128 : (t + 1) * 128] = moved[8 : 8 + rows, t * 128 : (t + 1) * 128]

    from_dn("i_up", ion.at[:, :, 0:8])
    from_up("i_dn", ion.at[:, :, 0:8])

    @pl.loop(0, n_rt, unroll=2)
    def _(c):
        row = pl.multiple_of(8 * c, 8)
        at = pl.ds(row, 8)
        for t in range(lt):
            de = -0.5 * (xn[t, pl.ds(row + 9, 8), :] - xn[t, pl.ds(row + 7, 8), :])
            dv = dnb[t, pl.ds(row + 8, 8), :]
            e_pos, e_neg = jnp.maximum(de, 0.0), jnp.minimum(de, 0.0)
            n_pos, n_neg = jnp.maximum(dv, 0.0), jnp.minimum(dv, 0.0)
            for s in range(3):
                n = ion[s, t, pl.ds(row + 8, 8), :]
                f = e_pos * ion_a[s, t, at, :] + e_neg * ion_b[s, t, at, :]
                f = f + n_pos * (n - ion[s, t, pl.ds(row + 7, 8), :])
                f = f + n_neg * (ion[s, t, pl.ds(row + 9, 8), :] - n)
                flux[s, t, at, :] = f

    arrived("max", mrx.at[0 : n_dev - 1])
    best = jnp.maximum(
        jnp.max(mrx[0 : n_dev - 1, :], axis=0, keepdims=True), mx[0:1, :]
    )
    best = jnp.max(best, axis=1, keepdims=True)
    step = jnp.broadcast_to(COURANT / (best + 1e-6), (8, 128))

    for s in range(3):
        scale = MOBILITY[s] * step

        @pl.loop(0, n_rt, unroll=2)
        def _(c):
            row = pl.multiple_of(8 * c, 8)
            for t in range(lt):
                upd_o[s, pl.ds(row, 8), t * 128 : (t + 1) * 128] = (
                    ion[s, t, pl.ds(row + 8, 8), :] - scale * flux[s, t, pl.ds(row, 8), :]
                )

    to_side = sig.at[:, 0 : 8 + 24 + GUARD + HALO]

    @pl.when(has_up)
    def _():
        sent("up", to_side)

    @pl.when(has_dn)
    def _():
        sent("dn", to_side)

    sent("sig", sig)
    sent("t", t_out)
    sent("lon", pk)
    sent("max", mrx.at[0 : n_dev - 1])


def write_out(pot_v, upd_v, pot_h, upd_h, sem):
    copies = [pltpu.make_async_copy(upd_v.at[s], upd_h.at[s], sem.at[s]) for s in range(3)]
    copies.append(pltpu.make_async_copy(pot_v, pot_h, sem.at[3]))
    for c in copies:
        c.start()
    for c in copies:
        c.wait()


def solution(mesh):
    nlat, nlon = mesh.shape["lat"], mesh.shape["lon"]

    def shards(pedersen, hall_conductivity, east_wind, north_wind, ion_density):
        lev, rows, cols = pedersen.shape
        lt = cols // 128
        nt = lt + 1
        width = nt * 128
        tall = rows + 2 * GUARD
        ext = rows + 2 * HALO
        groups = PIECES + 2
        vm = lambda *shape: pltpu.VMEM(shape, F32)
        half = lambda *shape: pltpu.VMEM(shape, BF16)
        dma = lambda *shape: pltpu.SemaphoreType.DMA(shape)
        hbm = pl.BlockSpec(memory_space=pltpu.HBM)
        vmem = pl.BlockSpec(memory_space=pltpu.VMEM)
        pot, upd = pl.pallas_call(
            functools.partial(kernel, nlat, nlon, lev, rows, lt),
            out_shape=(pltpu.VMEM((rows, cols), F32), pltpu.VMEM((3, rows, cols), F32)),
            in_specs=[hbm] * 5,
            out_specs=(vmem, vmem),
            scratch_shapes=[vm(4, lev, rows, cols)]
            + [vm(3, lt, rows + 16, 128)] + [vm(3, lt, rows, 128)] * 2
            + [vm(lt, rows, 128), vm(lt, rows, 128), vm(lt, rows + 16, 128)]
            + [vm(lt, rows, 128)] * 4
            + [vm(nt, tall, 128)] * 2
            + [vm(4 + 4 * groups, 8, 128)] + [vm(2, 1, 8, 128)] * 2 + [vm(2, groups, 8, 128)] * 2
            + [half(tall, 3 * width), half(3 * width, width), half(3 * width, 2 * lt * 128)]
            + [pltpu.SMEM((2, SWEEPS), F32)]
            + [vm(nt, tall, 128)] * 2
            + [vm(nt, ext, 128)] * 5
            + [vm(2, nt, ext, 128), vm(nt, ext + 16, 128)]
            + [vm(lt, rows + 16, 128)] * 2
            + [vm(3, lt, rows, 128), vm(8, 128), vm(nlat * nlon, 128)]
            + [dma(len(in_groups(rows // 8))), dma(1), dma(len(SEND)), dma(len(RECV))],
            compiler_params=pltpu.CompilerParams(
                collective_id=0, has_side_effects=True, vmem_limit_bytes=60 * 1024 * 1024
            ),
        )(pedersen, hall_conductivity, east_wind, north_wind, ion_density)
        pot = pltpu.with_memory_space_constraint(pot, pltpu.VMEM)
        upd = pltpu.with_memory_space_constraint(upd, pltpu.VMEM)
        return pl.pallas_call(
            write_out,
            out_shape=(
                jax.ShapeDtypeStruct((rows, cols), F32),
                jax.ShapeDtypeStruct((3, rows, cols), F32),
            ),
            in_specs=[vmem, vmem],
            out_specs=(hbm, hbm),
            scratch_shapes=[dma(4)],
        )(pot, upd)

    spec = P(None, "lat", "lon")
    return jax.shard_map(
        shards,
        mesh=mesh,
        in_specs=(spec,) * 5,
        out_specs=(P("lat", "lon"), spec),
        check_vma=False,
    )
```

time: 58.7 us -> 53.3 us (0.908)
  Pallas kernels: 56.3 us -> 52.6 us
  local copies, waits for them, and re-layouts: 1.58 us -> 0 us
    pallas_call x1, Pallas kernels: 56.3 us -> 51.6 us  [shards(): pl.pallas_call(functools.partial(kernel, nlat, nlon, lev, rows, lt), out_...]
    unnamed x2 -> x0, local copies, waits for them, and re-layouts: 1.58 us -> none
    pallas_call x0 -> x1, Pallas kernels: none -> 1 us  [shards(): pl.pallas_call(write_out, out_shape=(jax.ShapeDtypeStruct((rows, cols), F...]
where the time goes in v1:
time: 53.3 us; the launch traced here: 53.2 us
  Pallas kernels  52.6 us (99%)
  between operations  0.64 us (1%)
    pallas_call x1, Pallas kernels, shards(): pl.pallas_call(functools.partial(kernel, nlat, nlon, lev, rows, lt), out_...  51.6 us

profile of v1, /device:TPU:0, one launch (start us, length us, event | category | flops | bytes accessed | tf_op | source)
XLA Modules:
  0.0 53.2 jit_solution(15690901863564095218)
XLA Ops:
  0.6 51.6 %shard_map.68 = (f32[128,512]{1,0:T(8,128)S(1)}, f32[3,128,512]{2,1,0:T(8,128)S(1)}) custom-call(f32[16,128,512]{2,1,0:T(8,128)} %ped_h.1, f32[16,128,512]{2,1,0:T(8,128)} %hall_h.1, f32[16,128,512]{2,1,0:T(8,128)} %east_h.1, f32[16,128,512]{2,1,0:T(8,128)} %north_h.1, f32[3,128,512]{2,1,0:T(8,128)} %ion_h.1), custom_call_target="tpu_custom_call" | custom-call | tf_op jit(solution)/shard_map/pallas_call | solution.py:608
  52.2 1.0 %shard_map.69 = (f32[128,512]{1,0:T(8,128)}, f32[3,128,512]{2,1,0:T(8,128)}) custom-call(f32[128,512]{1,0:T(8,128)S(1)} %get-tuple-element.4.pot_v, f32[3,128,512]{2,1,0:T(8,128)S(1)} %get-tuple-element.5.upd_v), custom_call_target="tpu_custom_call" | custom-call | tf_op jit(solution)/shard_map/pallas_call | solution.py:633

commit v2 on v1

--- a/solution.py
+++ b/solution.py
@@ -37,8 +37,9 @@
 
 
 RECV = ("e", "ion", "n_up", "n_dn", "i_up", "i_dn", "sig_a", "sig_b", "t_a", "t_b", "t_c",
-        "s_up", "s_dn", "s_lon", "v_up", "v_dn", "v_lon", "v_last", "max")
-SEND = ("sig", "t", "lon", "up", "dn", "max")
+        "s_up", "s_dn", "s_lo", "s_hi", "s_lon", "v_up", "v_dn", "v_lo", "v_hi", "v_lon",
+        "inner", "max")
+SEND = ("sig", "t", "lon", "up", "dn", "up_lon", "dn_lon", "max")
 EDGE = 32
 
 
@@ -57,7 +58,7 @@
     pot_o, upd_o,
     vin, ion, ion_a, ion_b,
     sig, cur_e, cur_n, s_one, t_out, sig_rx, t_rx,
-    S, src, pk, rx_e, rx_ion, rx_s, rx_v,
+    S, src, pk, rx_e, rx_ion, rx_s, rx_v, rx_in,
     lhs, to_strided, to_plain, coef,
     SP, U, SR, rR, mR, invR, spR, X, xr, xn, dnb,
     flux, mx, mrx,
@@ -77,6 +78,7 @@
     lf = (me_lat, lax.rem(me_lon + nlon - 1, nlon))
     rt = (me_lat, lax.rem(me_lon + 1, nlon))
     mirror = (nlat - 1 - me_lat, me_lon)
+    far_lf, far_rt = (mirror[0], lf[1]), (mirror[0], rt[1])
     others = [
         (lax.rem(me_lat + a, nlat), lax.rem(me_lon + b, nlon))
         for a in range(nlat) for b in range(nlon) if a or b
@@ -271,8 +273,24 @@
                 d_lat = 0.5 * (cur_n[t, row + 9 : row + 17, :] - cur_n[t, row + 7 : row + 15, :])
                 s_one[t, at, :] = d_lon + d_lat
                 t_out[t, at, :] = d_lon - d_lat
-        if q in (0, PIECES - 1):
-            send_t(q, "t_a")
+
+    outer, inner = [0, PIECES - 1], list(range(1, PIECES - 1))
+    slot_s = 4
+    slot_v = slot_s + 2 * PIECES
+    slot_in = slot_v + 2 * len(outer)
+    slot_far = slot_in + 2 * len(inner)
+    slot_corner = slot_far + 2 * len(inner)
+    for i, q in enumerate(inner):
+        home = [8 * (q * per + k) for k in range(per)]
+        for side, t in enumerate((0, lt - 1)):
+            near_slot, far_slot = slot_in + 2 * i + side, slot_far + 2 * i + side
+            pack(near_slot, [s_one[t, r : r + 8, :] for r in home], EDGE, side * EDGE)
+            pack(far_slot, [t_out[t, r : r + 8, :] for r in home[::-1]], EDGE, side * EDGE)
+            there, mine = len(inner) - 1 - i, i
+            rcopy(pk.at[near_slot], rx_in.at[side, 0, mine], (lf, rt)[side], "lon", "inner").start()
+            rcopy(
+                pk.at[far_slot], rx_in.at[side, 1, there], (far_lf, far_rt)[side], "lon", "inner"
+            ).start()
 
     for j in range(nt):
         @pl.loop(0, 8, unroll=2)
@@ -317,43 +335,65 @@
 
     def spread_piece(out, rx, slot, q, recv):
         p = PIECES - 1 - q
-        spread(out, rx, slot + 2 * p, p, GUARD + p * per * 8, per, recv)
+        spread(out, rx, slot, p, GUARD + p * per * 8, per, recv)
 
     def gather_piece(out, rx, q):
         p = PIECES - 1 - q
         gather(out, rx, p, GUARD + p * per * 8, per)
 
-    def lat_send(out, depth, name):
+    def lat_send(out, rx, depth, name, slot):
         lo, hi = GUARD, GUARD + rows
         to_up(out.at[0:lt, lo : lo + depth], out.at[0:lt, hi : hi + depth], name + "_up")
         to_dn(out.at[0:lt, hi - depth : hi], out.at[0:lt, lo - depth : lo], name + "_dn")
-
-    def lat_spread(out, rx, depth, name, slot):
+        for edge, first in enumerate((lo, hi - depth)):
+            for side, t in enumerate((0, lt - 1)):
+                tiles = [out[t, r : r + 8, :] for r in range(first, first + depth, 8)]
+                pack(slot + 2 * edge + side, tiles, EDGE, side * EDGE)
+
+        def corners(edge, lat, send, recv):
+            for side, lon in enumerate((lf[1], rt[1])):
+                rcopy(
+                    pk.at[slot + 2 * edge + side], rx.at[side, PIECES + 1 - edge], (lat, lon),
+                    send, recv,
+                ).start()
+
+        @pl.when(has_up)
+        def _():
+            corners(0, up[0], "up_lon", name + "_hi")
+
+        @pl.when(has_dn)
+        def _():
+            corners(1, dn[0], "dn_lon", name + "_lo")
+
+    def lat_gather(out, rx, depth, name):
         lo, hi = GUARD, GUARD + rows
-        from_up(name + "_dn", out.at[0:lt, lo - depth : lo])
-        spread(out, rx, slot + 2 * PIECES, PIECES, lo - depth, depth // 8, name + "_lon")
-        from_dn(name + "_up", out.at[0:lt, lo - depth : lo])
-        spread(out, rx, slot + 2 * PIECES + 2, PIECES + 1, hi, depth // 8, name + "_lon")
-
-    def lat_gather(out, rx, depth):
-        gather(out, rx, PIECES, GUARD - depth, depth // 8)
-        gather(out, rx, PIECES + 1, GUARD + rows, depth // 8)
-
-    outer, inner = [0, PIECES - 1], list(range(1, PIECES - 1))
-    slot_s, slot_v = 4, 4 + 2 * (PIECES + 2)
+
+        @pl.when(has_up)
+        def _():
+            arrived(name + "_dn", out.at[0:lt, lo - depth : lo])
+            arrived(name + "_lo", pk.at[0:2])
+            gather(out, rx, PIECES, lo - depth, depth // 8)
+
+        @pl.when(has_dn)
+        def _():
+            arrived(name + "_up", out.at[0:lt, lo - depth : lo])
+            arrived(name + "_hi", pk.at[0:2])
+            gather(out, rx, PIECES + 1, hi, depth // 8)
 
     arrived("sig_a", sig_rx.at[:, 0 : 2 * per * 8])
     for q in outer:
         combine(sig, sig_rx, S, q)
-    lat_send(S, GUARD, "s")
+    lat_send(S, rx_s, GUARD, "s", slot_corner)
+    for q in outer:
+        send_t(q, "t_a")
     for q in inner[:-1]:
         send_t(q, "t_b")
-    for q in outer:
-        spread_piece(S, rx_s, slot_s, q, "s_lon")
+    for i, q in enumerate(outer):
+        spread_piece(S, rx_s, slot_s + 2 * i, q, "s_lon")
     arrived("sig_b", sig_rx.at[:, 0 : (PIECES - 2) * per * 8])
-    for q in inner:
+    for i, q in enumerate(inner):
         combine(sig, sig_rx, S, q)
-        spread_piece(S, rx_s, slot_s, q, "s_lon")
+        spread_piece(S, rx_s, slot_s + 4 + 2 * i, q, "s_lon")
 
     arrived("ion", rx_ion)
     i_fr, i_fl = rx_ion[0, 0, :, :], rx_ion[1, 0, :, :]
@@ -365,11 +405,20 @@
             ion_a[s, t, at, :] = tiles[t] - left[t]
             ion_b[s, t, at, :] = right[t] - tiles[t]
 
-    lat_spread(S, rx_s, GUARD, "s", slot_s)
-    arrived("s_lon", rx_s)
+    arrived("t_a", t_rx.at[:, 0 : 2 * per * 8])
+    for q in outer:
+        combine(s_one, t_rx, src, q)
+    lat_send(src, rx_v, HALO, "v", slot_corner + 4)
+    send_t(inner[-1], "t_c")
+    to_up(ion.at[:, :, 8:16], ion.at[:, :, rows + 8 : rows + 16], "i_up")
+    to_dn(ion.at[:, :, rows : rows + 8], ion.at[:, :, 0:8], "i_dn")
+    for i, q in enumerate(outer):
+        spread_piece(src, rx_v, slot_v + 2 * i, q, "v_lon")
+
+    arrived("s_lon", rx_s.at[:, 0:PIECES])
     for q in outer + inner:
         gather_piece(S, rx_s, q)
-    lat_gather(S, rx_s, GUARD)
+    lat_gather(S, rx_s, GUARD, "s")
 
     def split(v, at, t):
         for part in range(3):
@@ -419,24 +468,22 @@
             mR[t, at, :] = (THETA - 1.0) - 8.0 * (quarter * s)
             X[1, t, at, :] = jnp.zeros((8, 128), F32)
 
-    arrived("t_a", t_rx.at[:, 0 : 2 * per * 8])
-    for q in outer:
-        combine(s_one, t_rx, src, q)
-    lat_send(src, HALO, "v")
-    send_t(inner[-1], "t_c")
-    to_up(ion.at[:, :, 8:16], ion.at[:, :, rows + 8 : rows + 16], "i_up")
-    to_dn(ion.at[:, :, rows : rows + 8], ion.at[:, :, 0:8], "i_dn")
-    for q in outer:
-        spread_piece(src, rx_v, slot_v, q, "v_lon")
+    def inner_edges(q):
+        p = PIECES - 1 - q
+        for side in range(2):
+            rx_v[side, p, :, :] = rx_in[side, 0, p - 1, :, :] + rev8(rx_in[side, 1, p - 1, :, :])
+        gather_piece(src, rx_v, q)
+
     arrived("t_b", t_rx.at[:, 0 : (PIECES - 3) * per * 8])
     for q in inner[:-1]:
         combine(s_one, t_rx, src, q)
-        spread_piece(src, rx_v, slot_v, q, "v_lon")
-    lat_spread(src, rx_v, HALO, "v", slot_v)
-    arrived("v_lon", pk.at[0 : 2 * (PIECES + 1)])
-    for q in outer + inner[:-1]:
+    arrived("inner", rx_in)
+    for q in inner:
+        inner_edges(q)
+    arrived("v_lon", pk.at[0 : 2 * len(outer)])
+    for q in outer:
         gather_piece(src, rx_v, q)
-    lat_gather(src, rx_v, HALO)
+    lat_gather(src, rx_v, HALO, "v")
     last = PIECES - 1 - inner[-1]
     last_lo, last_hi = HALO + last * per * 8, HALO + (last + 1) * per * 8
     for lo, hi in ((0, last_lo), (last_hi, ext)):
@@ -447,9 +494,6 @@
 
     arrived("t_c", t_rx.at[:, 0 : per * 8])
     combine(s_one, t_rx, src, inner[-1])
-    spread_piece(src, rx_v, slot_v, inner[-1], "v_last")
-    arrived("v_last", pk.at[0:2])
-    gather_piece(src, rx_v, inner[-1])
     split_rows(src, skip, last_lo, last_hi)
     moved = jnp.dot(lhs[last_lo:last_hi, :], to_strided[...], preferred_element_type=F32)
     for t in range(nt):
@@ -569,14 +613,16 @@
     @pl.when(has_up)
     def _():
         sent("up", to_side)
+        sent("up_lon", pk.at[0:4])
 
     @pl.when(has_dn)
     def _():
         sent("dn", to_side)
+        sent("dn_lon", pk.at[0:4])
 
     sent("sig", sig)
     sent("t", t_out)
-    sent("lon", pk)
+    sent("lon", pk.at[0:slot_corner])
     sent("max", mrx.at[0 : n_dev - 1])
 
 
@@ -615,7 +661,8 @@
             + [vm(lt, rows, 128), vm(lt, rows, 128), vm(lt, rows + 16, 128)]
             + [vm(lt, rows, 128)] * 4
             + [vm(nt, tall, 128)] * 2
-            + [vm(4 + 4 * groups, 8, 128)] + [vm(2, 1, 8, 128)] * 2 + [vm(2, groups, 8, 128)] * 2
+            + [vm(8 * PIECES, 8, 128)] + [vm(2, 1, 8, 128)] * 2 + [vm(2, groups, 8, 128)] * 2
+            + [vm(2, 2, PIECES - 2, 8, 128)]
             + [half(tall, 3 * width), half(3 * width, width), half(3 * width, 2 * lt * 128)]
             + [pltpu.SMEM((2, SWEEPS), F32)]
             + [vm(nt, tall, 128)] * 2

time: 53.3 us -> 46.3 us (0.87)
  Pallas kernels: 52.6 us -> 45.5 us
    pallas_call x1, Pallas kernels: 51.6 us -> 44.5 us  [shards(): pl.pallas_call(functools.partial(kernel, nlat, nlon, lev, rows, lt), out_...]
where the time goes in v2:
time: 46.3 us; the launch traced here: 46.2 us
  Pallas kernels  45.5 us (98%)
  between operations  0.64 us (1%)
    pallas_call x1, Pallas kernels, shards(): pl.pallas_call(functools.partial(kernel, nlat, nlon, lev, rows, lt), out_...  44.5 us
    pallas_call x1, Pallas kernels, shards(): pl.pallas_call(write_out, out_shape=(jax.ShapeDtypeStruct((rows, cols), F...  1 us

profile of v2, /device:TPU:0, one launch (start us, length us, event | category | flops | bytes accessed | tf_op | source)
XLA Modules:
  0.0 46.2 jit_solution(1706750179547310562)
XLA Ops:
  0.6 44.5 %shard_map.68 = (f32[128,512]{1,0:T(8,128)S(1)}, f32[3,128,512]{2,1,0:T(8,128)S(1)}) custom-call(f32[16,128,512]{2,1,0:T(8,128)} %ped_h.1, f32[16,128,512]{2,1,0:T(8,128)} %hall_h.1, f32[16,128,512]{2,1,0:T(8,128)} %east_h.1, f32[16,128,512]{2,1,0:T(8,128)} %north_h.1, f32[3,128,512]{2,1,0:T(8,128)} %ion_h.1), custom_call_target="tpu_custom_call" | custom-call | tf_op jit(solution)/shard_map/pallas_call | solution.py:654
  45.2 1.0 %shard_map.69 = (f32[128,512]{1,0:T(8,128)}, f32[3,128,512]{2,1,0:T(8,128)}) custom-call(f32[128,512]{1,0:T(8,128)S(1)} %get-tuple-element.4.pot_v, f32[3,128,512]{2,1,0:T(8,128)S(1)} %get-tuple-element.5.upd_v), custom_call_target="tpu_custom_call" | custom-call | tf_op jit(solution)/shard_map/pallas_call | solution.py:680

commit v3 on v2

--- a/solution.py
+++ b/solution.py
@@ -38,7 +38,7 @@
 
 RECV = ("e", "ion", "n_up", "n_dn", "i_up", "i_dn", "sig_a", "sig_b", "t_a", "t_b", "t_c",
         "s_up", "s_dn", "s_lo", "s_hi", "s_lon", "v_up", "v_dn", "v_lo", "v_hi", "v_lon",
-        "inner", "max")
+        "inner", "inner_s", "max")
 SEND = ("sig", "t", "lon", "up", "dn", "up_lon", "dn_lon", "max")
 EDGE = 32
 
@@ -58,7 +58,7 @@
     pot_o, upd_o,
     vin, ion, ion_a, ion_b,
     sig, cur_e, cur_n, s_one, t_out, sig_rx, t_rx,
-    S, src, pk, rx_e, rx_ion, rx_s, rx_v, rx_in,
+    S, src, pk, rx_e, rx_ion, rx_s, rx_v, rx_in, rx_ins,
     lhs, to_strided, to_plain, coef,
     SP, U, SR, rR, mR, invR, spR, X, xr, xn, dnb,
     flux, mx, mrx,
@@ -227,7 +227,6 @@
     for q in range(1, PIECES - 1):
         columns(2 * q + 2)
         columns(2 * q + 3)
-        send_sig(q, "sig_b")
 
     step_e = 128 // n_rt
     pack(0, [cur_e[0, 8 * c : 8 * c + 8, :] for c in range(n_rt)], step_e, 0)
@@ -255,6 +254,25 @@
     pack(2, [ion[s, 0, 8 * c + 8 : 8 * c + 16, :] for s, c in bands], step_i, 0)
     pack(3, [ion[s, lt - 1, 8 * c + 8 : 8 * c + 16, :] for s, c in bands], step_i, 1)
     send_lon(2, rx_ion, 0, "ion")
+
+    outer, inner = [0, PIECES - 1], list(range(1, PIECES - 1))
+    slot_s = 4
+    slot_v = slot_s + 2 * PIECES
+    slot_in = slot_v + 2 * len(outer)
+    slot_far = slot_in + 2 * len(inner)
+    slot_fars = slot_far + 2 * len(inner)
+    slot_corner = slot_fars + 2 * len(inner)
+
+    def two_terms(own, other, rx, slot, far, recv):
+        for i, q in enumerate(inner):
+            home = [8 * (q * per + k) for k in range(per)]
+            for side, t in enumerate((0, lt - 1)):
+                a, b = slot + 2 * i + side, far + 2 * i + side
+                pack(a, [own[t, r : r + 8, :] for r in home], EDGE, side * EDGE)
+                pack(b, [other[t, r : r + 8, :] for r in home[::-1]], EDGE, side * EDGE)
+                there = len(inner) - 1 - i
+                rcopy(pk.at[a], rx.at[side, 0, i], (lf, rt)[side], "lon", recv).start()
+                rcopy(pk.at[b], rx.at[side, 1, there], (far_lf, far_rt)[side], "lon", recv).start()
 
     from_dn("n_up", cur_n.at[:, 0:8])
     from_up("n_dn", cur_n.at[:, 0:8])
@@ -273,24 +291,14 @@
                 d_lat = 0.5 * (cur_n[t, row + 9 : row + 17, :] - cur_n[t, row + 7 : row + 15, :])
                 s_one[t, at, :] = d_lon + d_lat
                 t_out[t, at, :] = d_lon - d_lat
-
-    outer, inner = [0, PIECES - 1], list(range(1, PIECES - 1))
-    slot_s = 4
-    slot_v = slot_s + 2 * PIECES
-    slot_in = slot_v + 2 * len(outer)
-    slot_far = slot_in + 2 * len(inner)
-    slot_corner = slot_far + 2 * len(inner)
-    for i, q in enumerate(inner):
-        home = [8 * (q * per + k) for k in range(per)]
-        for side, t in enumerate((0, lt - 1)):
-            near_slot, far_slot = slot_in + 2 * i + side, slot_far + 2 * i + side
-            pack(near_slot, [s_one[t, r : r + 8, :] for r in home], EDGE, side * EDGE)
-            pack(far_slot, [t_out[t, r : r + 8, :] for r in home[::-1]], EDGE, side * EDGE)
-            there, mine = len(inner) - 1 - i, i
-            rcopy(pk.at[near_slot], rx_in.at[side, 0, mine], (lf, rt)[side], "lon", "inner").start()
-            rcopy(
-                pk.at[far_slot], rx_in.at[side, 1, there], (far_lf, far_rt)[side], "lon", "inner"
-            ).start()
+        if q in outer:
+            send_t(q, "t_a")
+        if q == outer[-1]:
+            for b in inner:
+                send_sig(b, "sig_b")
+            two_terms(sig, sig, rx_ins, slot_s + 2 * len(outer), slot_fars, "inner_s")
+
+    two_terms(s_one, t_out, rx_in, slot_in, slot_far, "inner")
 
     for j in range(nt):
         @pl.loop(0, 8, unroll=2)
@@ -380,21 +388,6 @@
             arrived(name + "_hi", pk.at[0:2])
             gather(out, rx, PIECES + 1, hi, depth // 8)
 
-    arrived("sig_a", sig_rx.at[:, 0 : 2 * per * 8])
-    for q in outer:
-        combine(sig, sig_rx, S, q)
-    lat_send(S, rx_s, GUARD, "s", slot_corner)
-    for q in outer:
-        send_t(q, "t_a")
-    for q in inner[:-1]:
-        send_t(q, "t_b")
-    for i, q in enumerate(outer):
-        spread_piece(S, rx_s, slot_s + 2 * i, q, "s_lon")
-    arrived("sig_b", sig_rx.at[:, 0 : (PIECES - 2) * per * 8])
-    for i, q in enumerate(inner):
-        combine(sig, sig_rx, S, q)
-        spread_piece(S, rx_s, slot_s + 4 + 2 * i, q, "s_lon")
-
     arrived("ion", rx_ion)
     i_fr, i_fl = rx_ion[0, 0, :, :], rx_ion[1, 0, :, :]
     for k, (s, c) in enumerate(bands):
@@ -405,18 +398,39 @@
             ion_a[s, t, at, :] = tiles[t] - left[t]
             ion_b[s, t, at, :] = right[t] - tiles[t]
 
+    arrived("sig_a", sig_rx.at[:, 0 : 2 * per * 8])
+    for q in outer:
+        combine(sig, sig_rx, S, q)
+    lat_send(S, rx_s, GUARD, "s", slot_corner)
+    for i, q in enumerate(outer):
+        spread_piece(S, rx_s, slot_s + 2 * i, q, "s_lon")
+
     arrived("t_a", t_rx.at[:, 0 : 2 * per * 8])
     for q in outer:
         combine(s_one, t_rx, src, q)
     lat_send(src, rx_v, HALO, "v", slot_corner + 4)
+    for q in inner[:-1]:
+        send_t(q, "t_b")
     send_t(inner[-1], "t_c")
     to_up(ion.at[:, :, 8:16], ion.at[:, :, rows + 8 : rows + 16], "i_up")
     to_dn(ion.at[:, :, rows : rows + 8], ion.at[:, :, 0:8], "i_dn")
     for i, q in enumerate(outer):
         spread_piece(src, rx_v, slot_v + 2 * i, q, "v_lon")
 
-    arrived("s_lon", rx_s.at[:, 0:PIECES])
-    for q in outer + inner:
+    def inner_edges(out, rx, pair, q):
+        p = PIECES - 1 - q
+        for side in range(2):
+            rx[side, p, :, :] = pair[side, 0, p - 1, :, :] + rev8(pair[side, 1, p - 1, :, :])
+        gather_piece(out, rx, q)
+
+    arrived("sig_b", sig_rx.at[:, 0 : (PIECES - 2) * per * 8])
+    for q in inner:
+        combine(sig, sig_rx, S, q)
+    arrived("inner_s", rx_ins)
+    for q in inner:
+        inner_edges(S, rx_s, rx_ins, q)
+    arrived("s_lon", pk.at[0 : 2 * len(outer)])
+    for q in outer:
         gather_piece(S, rx_s, q)
     lat_gather(S, rx_s, GUARD, "s")
 
@@ -468,18 +482,12 @@
             mR[t, at, :] = (THETA - 1.0) - 8.0 * (quarter * s)
             X[1, t, at, :] = jnp.zeros((8, 128), F32)
 
-    def inner_edges(q):
-        p = PIECES - 1 - q
-        for side in range(2):
-            rx_v[side, p, :, :] = rx_in[side, 0, p - 1, :, :] + rev8(rx_in[side, 1, p - 1, :, :])
-        gather_piece(src, rx_v, q)
-
     arrived("t_b", t_rx.at[:, 0 : (PIECES - 3) * per * 8])
     for q in inner[:-1]:
         combine(s_one, t_rx, src, q)
     arrived("inner", rx_in)
     for q in inner:
-        inner_edges(q)
+        inner_edges(src, rx_v, rx_in, q)
     arrived("v_lon", pk.at[0 : 2 * len(outer)])
     for q in outer:
         gather_piece(src, rx_v, q)
@@ -661,8 +669,8 @@
             + [vm(lt, rows, 128), vm(lt, rows, 128), vm(lt, rows + 16, 128)]
             + [vm(lt, rows, 128)] * 4
             + [vm(nt, tall, 128)] * 2
-            + [vm(8 * PIECES, 8, 128)] + [vm(2, 1, 8, 128)] * 2 + [vm(2, groups, 8, 128)] * 2
-            + [vm(2, 2, PIECES - 2, 8, 128)]
+            + [vm(10 * PIECES - 4, 8, 128)] + [vm(2, 1, 8, 128)] * 2 + [vm(2, groups, 8, 128)] * 2
+            + [vm(2, 2, PIECES - 2, 8, 128)] * 2
             + [half(tall, 3 * width), half(3 * width, width), half(3 * width, 2 * lt * 128)]
             + [pltpu.SMEM((2, SWEEPS), F32)]
             + [vm(nt, tall, 128)] * 2

time: 46.3 us -> 45.6 us (0.985)
  Pallas kernels: 45.5 us -> 44.8 us
    pallas_call x1, Pallas kernels: 44.5 us -> 43.8 us  [shards(): pl.pallas_call(functools.partial(kernel, nlat, nlon, lev, rows, lt), out_...]
where the time goes in v3:
time: 45.6 us; the launch traced here: 45.4 us
  Pallas kernels  44.8 us (98%)
  between operations  0.64 us (1%)
    pallas_call x1, Pallas kernels, shards(): pl.pallas_call(functools.partial(kernel, nlat, nlon, lev, rows, lt), out_...  43.8 us
    pallas_call x1, Pallas kernels, shards(): pl.pallas_call(write_out, out_shape=(jax.ShapeDtypeStruct((rows, cols), F...  1 us

profile of v3, /device:TPU:0, one launch (start us, length us, event | category | flops | bytes accessed | tf_op | source)
XLA Modules:
  0.0 45.4 jit_solution(6714523023284447629)
XLA Ops:
  0.6 43.8 %shard_map.68 = (f32[128,512]{1,0:T(8,128)S(1)}, f32[3,128,512]{2,1,0:T(8,128)S(1)}) custom-call(f32[16,128,512]{2,1,0:T(8,128)} %ped_h.1, f32[16,128,512]{2,1,0:T(8,128)} %hall_h.1, f32[16,128,512]{2,1,0:T(8,128)} %east_h.1, f32[16,128,512]{2,1,0:T(8,128)} %north_h.1, f32[3,128,512]{2,1,0:T(8,128)} %ion_h.1), custom_call_target="tpu_custom_call" | custom-call | tf_op jit(solution)/shard_map/pallas_call | solution.py:662
  44.4 1.0 %shard_map.69 = (f32[128,512]{1,0:T(8,128)}, f32[3,128,512]{2,1,0:T(8,128)}) custom-call(f32[128,512]{1,0:T(8,128)S(1)} %get-tuple-element.4.pot_v, f32[3,128,512]{2,1,0:T(8,128)S(1)} %get-tuple-element.5.upd_v), custom_call_target="tpu_custom_call" | custom-call | tf_op jit(solution)/shard_map/pallas_call | solution.py:688

commit v4 on v3

--- a/solution.py
+++ b/solution.py
@@ -36,7 +36,7 @@
     return first_list, second_list
 
 
-RECV = ("e", "ion", "n_up", "n_dn", "i_up", "i_dn", "sig_a", "sig_b", "t_a", "t_b", "t_c",
+RECV = ("e", "ion", "n_up", "n_dn", "i_up", "i_dn", "sig_a", "sig_b", "t_a", "t_b",
         "s_up", "s_dn", "s_lo", "s_hi", "s_lon", "v_up", "v_dn", "v_lo", "v_hi", "v_lon",
         "inner", "inner_s", "max")
 SEND = ("sig", "t", "lon", "up", "dn", "up_lon", "dn_lon", "max")
@@ -218,8 +218,8 @@
     columns(0)
     columns(1)
     pl.semaphore_wait(barrier, n_dev - 1)
-    to_up(cur_n.at[:, 8:16], cur_n.at[:, rows + 8 : rows + 16], "n_up")
-    to_dn(cur_n.at[:, rows : rows + 8], cur_n.at[:, 0:8], "n_dn")
+    to_up(cur_n.at[:, 8:9], cur_n.at[:, rows + 8 : rows + 9], "n_up")
+    to_dn(cur_n.at[:, rows + 7 : rows + 8], cur_n.at[:, 7:8], "n_dn")
     columns(2)
     send_sig(0, "sig_a")
     columns(3)
@@ -227,11 +227,39 @@
     for q in range(1, PIECES - 1):
         columns(2 * q + 2)
         columns(2 * q + 3)
+        if q != PIECES - 2:
+            send_sig(q, "sig_b")
 
     step_e = 128 // n_rt
     pack(0, [cur_e[0, 8 * c : 8 * c + 8, :] for c in range(n_rt)], step_e, 0)
     pack(1, [cur_e[lt - 1, 8 * c : 8 * c + 8, :] for c in range(n_rt)], step_e, 1)
     send_lon(0, rx_e, 0, "e")
+
+    outer, inner = [0, PIECES - 1], list(range(1, PIECES - 1))
+    slot_s = 4
+    slot_fars = slot_s + 2 * PIECES
+    slot_v = slot_fars + 2 * len(inner)
+    slot_in = slot_v + 2 * len(outer)
+    slot_far = slot_in + 2
+    slot_corner = slot_far + 2
+
+    def two_terms(own, other, rx, slot, far, runs, edge, recv):
+        for i, (lo, hi) in enumerate(runs):
+            there = runs.index((n_rt - hi, n_rt - lo))
+            for side, t in enumerate((0, lt - 1)):
+                a, b = slot + 2 * i + side, far + 2 * i + side
+                pack(a, [own[t, 8 * k : 8 * k + 8, :] for k in range(lo, hi)], edge, side * edge)
+                pack(
+                    b, [other[t, 8 * k : 8 * k + 8, :] for k in range(lo, hi)][::-1],
+                    edge, side * edge,
+                )
+                rcopy(pk.at[a], rx.at[side, 0, i], (lf, rt)[side], "lon", recv).start()
+                rcopy(pk.at[b], rx.at[side, 1, there], (far_lf, far_rt)[side], "lon", recv).start()
+
+    two_terms(
+        sig, sig, rx_ins, slot_s + 2 * len(outer), slot_fars,
+        [(q * per, (q + 1) * per) for q in inner], EDGE, "inner_s",
+    )
 
     @pl.when(jnp.logical_not(has_up))
     def _():
@@ -255,27 +283,8 @@
     pack(3, [ion[s, lt - 1, 8 * c + 8 : 8 * c + 16, :] for s, c in bands], step_i, 1)
     send_lon(2, rx_ion, 0, "ion")
 
-    outer, inner = [0, PIECES - 1], list(range(1, PIECES - 1))
-    slot_s = 4
-    slot_v = slot_s + 2 * PIECES
-    slot_in = slot_v + 2 * len(outer)
-    slot_far = slot_in + 2 * len(inner)
-    slot_fars = slot_far + 2 * len(inner)
-    slot_corner = slot_fars + 2 * len(inner)
-
-    def two_terms(own, other, rx, slot, far, recv):
-        for i, q in enumerate(inner):
-            home = [8 * (q * per + k) for k in range(per)]
-            for side, t in enumerate((0, lt - 1)):
-                a, b = slot + 2 * i + side, far + 2 * i + side
-                pack(a, [own[t, r : r + 8, :] for r in home], EDGE, side * EDGE)
-                pack(b, [other[t, r : r + 8, :] for r in home[::-1]], EDGE, side * EDGE)
-                there = len(inner) - 1 - i
-                rcopy(pk.at[a], rx.at[side, 0, i], (lf, rt)[side], "lon", recv).start()
-                rcopy(pk.at[b], rx.at[side, 1, there], (far_lf, far_rt)[side], "lon", recv).start()
-
-    from_dn("n_up", cur_n.at[:, 0:8])
-    from_up("n_dn", cur_n.at[:, 0:8])
+    from_dn("n_up", cur_n.at[:, 7:8])
+    from_up("n_dn", cur_n.at[:, 7:8])
     arrived("e", rx_e)
     e_fr, e_fl = rx_e[0, 0, :, :], rx_e[1, 0, :, :]
     for q in [0, PIECES - 1] + list(range(1, PIECES - 1)):
@@ -293,12 +302,10 @@
                 t_out[t, at, :] = d_lon - d_lat
         if q in outer:
             send_t(q, "t_a")
-        if q == outer[-1]:
-            for b in inner:
-                send_sig(b, "sig_b")
-            two_terms(sig, sig, rx_ins, slot_s + 2 * len(outer), slot_fars, "inner_s")
-
-    two_terms(s_one, t_out, rx_in, slot_in, slot_far, "inner")
+    send_sig(PIECES - 2, "sig_b")
+    mid = (per, n_rt - per)
+    edge_in = 128 // (mid[1] - mid[0])
+    two_terms(s_one, t_out, rx_in, slot_in, slot_far, [mid], edge_in, "inner")
 
     for j in range(nt):
         @pl.loop(0, 8, unroll=2)
@@ -333,13 +340,15 @@
         pack(slot + 1, tiles(lt - 1), EDGE, EDGE)
         send_lon(slot, rx, g, recv)
 
+    def unpack(out, fr, fl, lo, count, edge):
+        for k in range(count):
+            a, b = turn(fr, 128 - edge * k), turn(fl, 256 - edge - edge * k)
+            out[lt, lo + 8 * k : lo + 8 * k + 8, :] = jnp.where(
+                lane < edge, a, jnp.where(lane >= 128 - edge, b, 0.0)
+            )
+
     def gather(out, rx, g, lo, count):
-        fr, fl = rx[0, g, :, :], rx[1, g, :, :]
-        for k in range(count):
-            a, b = turn(fr, 128 - EDGE * k), turn(fl, 256 - EDGE - EDGE * k)
-            out[lt, lo + 8 * k : lo + 8 * k + 8, :] = jnp.where(
-                lane < EDGE, a, jnp.where(lane >= 128 - EDGE, b, 0.0)
-            )
+        unpack(out, rx[0, g, :, :], rx[1, g, :, :], lo, count, EDGE)
 
     def spread_piece(out, rx, slot, q, recv):
         p = PIECES - 1 - q
@@ -409,26 +418,23 @@
     for q in outer:
         combine(s_one, t_rx, src, q)
     lat_send(src, rx_v, HALO, "v", slot_corner + 4)
-    for q in inner[:-1]:
+    for q in inner:
         send_t(q, "t_b")
-    send_t(inner[-1], "t_c")
-    to_up(ion.at[:, :, 8:16], ion.at[:, :, rows + 8 : rows + 16], "i_up")
-    to_dn(ion.at[:, :, rows : rows + 8], ion.at[:, :, 0:8], "i_dn")
+    to_up(ion.at[:, :, 8:9], ion.at[:, :, rows + 8 : rows + 9], "i_up")
+    to_dn(ion.at[:, :, rows + 7 : rows + 8], ion.at[:, :, 7:8], "i_dn")
     for i, q in enumerate(outer):
         spread_piece(src, rx_v, slot_v + 2 * i, q, "v_lon")
 
-    def inner_edges(out, rx, pair, q):
-        p = PIECES - 1 - q
-        for side in range(2):
-            rx[side, p, :, :] = pair[side, 0, p - 1, :, :] + rev8(pair[side, 1, p - 1, :, :])
-        gather_piece(out, rx, q)
+    def inner_edges(out, pair, i, lo, count, edge):
+        fr, fl = [pair[side, 0, i, :, :] + rev8(pair[side, 1, i, :, :]) for side in range(2)]
+        unpack(out, fr, fl, GUARD + 8 * lo, count, edge)
 
     arrived("sig_b", sig_rx.at[:, 0 : (PIECES - 2) * per * 8])
     for q in inner:
         combine(sig, sig_rx, S, q)
     arrived("inner_s", rx_ins)
-    for q in inner:
-        inner_edges(S, rx_s, rx_ins, q)
+    for i, q in enumerate(inner):
+        inner_edges(S, rx_ins, i, q * per, per, EDGE)
     arrived("s_lon", pk.at[0 : 2 * len(outer)])
     for q in outer:
         gather_piece(S, rx_s, q)
@@ -482,30 +488,25 @@
             mR[t, at, :] = (THETA - 1.0) - 8.0 * (quarter * s)
             X[1, t, at, :] = jnp.zeros((8, 128), F32)
 
-    arrived("t_b", t_rx.at[:, 0 : (PIECES - 3) * per * 8])
-    for q in inner[:-1]:
-        combine(s_one, t_rx, src, q)
-    arrived("inner", rx_in)
-    for q in inner:
-        inner_edges(src, rx_v, rx_in, q)
+    def transform(lo, hi):
+        split_rows(src, skip, lo, hi)
+        moved = jnp.dot(lhs[lo:hi, :], to_strided[...], preferred_element_type=F32)
+        for t in range(nt):
+            SP[t, lo:hi, :] = moved[:, t * 128 : (t + 1) * 128]
+
     arrived("v_lon", pk.at[0 : 2 * len(outer)])
     for q in outer:
         gather_piece(src, rx_v, q)
     lat_gather(src, rx_v, HALO, "v")
-    last = PIECES - 1 - inner[-1]
-    last_lo, last_hi = HALO + last * per * 8, HALO + (last + 1) * per * 8
-    for lo, hi in ((0, last_lo), (last_hi, ext)):
-        split_rows(src, skip, lo, hi)
-        moved = jnp.dot(lhs[lo:hi, :], to_strided[...], preferred_element_type=F32)
-        for t in range(nt):
-            SP[t, lo:hi, :] = moved[:, t * 128 : (t + 1) * 128]
-
-    arrived("t_c", t_rx.at[:, 0 : per * 8])
-    combine(s_one, t_rx, src, inner[-1])
-    split_rows(src, skip, last_lo, last_hi)
-    moved = jnp.dot(lhs[last_lo:last_hi, :], to_strided[...], preferred_element_type=F32)
-    for t in range(nt):
-        SP[t, last_lo:last_hi, :] = moved[:, t * 128 : (t + 1) * 128]
+    late_lo, late_hi = HALO + 8 * mid[0], HALO + 8 * mid[1]
+    transform(0, late_lo)
+    transform(late_hi, ext)
+    arrived("inner", rx_in)
+    inner_edges(src, rx_in, 0, mid[0], mid[1] - mid[0], edge_in)
+    arrived("t_b", t_rx.at[:, 0 : 8 * (mid[1] - mid[0])])
+    for q in inner:
+        combine(s_one, t_rx, src, q)
+    transform(late_lo, late_hi)
     for c in range(R):
         at = slice(8 * c, 8 * c + 8)
         for t in range(nt):
@@ -579,8 +580,8 @@
         dnb[t, :, :] = moved[:, (lt + t) * 128 : (lt + t + 1) * 128]
         pot_o[:, t * 128 : (t + 1) * 128] = moved[8 : 8 + rows, t * 128 : (t + 1) * 128]
 
-    from_dn("i_up", ion.at[:, :, 0:8])
-    from_up("i_dn", ion.at[:, :, 0:8])
+    from_dn("i_up", ion.at[:, :, 7:8])
+    from_up("i_dn", ion.at[:, :, 7:8])
 
     @pl.loop(0, n_rt, unroll=2)
     def _(c):
@@ -616,7 +617,7 @@
                     ion[s, t, pl.ds(row + 8, 8), :] - scale * flux[s, t, pl.ds(row, 8), :]
                 )
 
-    to_side = sig.at[:, 0 : 8 + 24 + GUARD + HALO]
+    to_side = sig.at[:, 0 : 1 + 3 + GUARD + HALO]
 
     @pl.when(has_up)
     def _():
@@ -669,8 +670,8 @@
             + [vm(lt, rows, 128), vm(lt, rows, 128), vm(lt, rows + 16, 128)]
             + [vm(lt, rows, 128)] * 4
             + [vm(nt, tall, 128)] * 2
-            + [vm(10 * PIECES - 4, 8, 128)] + [vm(2, 1, 8, 128)] * 2 + [vm(2, groups, 8, 128)] * 2
-            + [vm(2, 2, PIECES - 2, 8, 128)] * 2
+            + [vm(8 * PIECES, 8, 128)] + [vm(2, 1, 8, 128)] * 2 + [vm(2, groups, 8, 128)] * 2
+            + [vm(2, 2, 1, 8, 128), vm(2, 2, PIECES - 2, 8, 128)]
             + [half(tall, 3 * width), half(3 * width, width), half(3 * width, 2 * lt * 128)]
             + [pltpu.SMEM((2, SWEEPS), F32)]
             + [vm(nt, tall, 128)] * 2

time: 45.6 us -> 45.2 us (level)
  no operation moved by 1% of the time
where the time goes in v4:
time: 45.2 us; the launch traced here: 45.1 us
  Pallas kernels  44.4 us (98%)
  between operations  0.64 us (1%)
    pallas_call x1, Pallas kernels, shards(): pl.pallas_call(functools.partial(kernel, nlat, nlon, lev, rows, lt), out_...  43.4 us
    pallas_call x1, Pallas kernels, shards(): pl.pallas_call(write_out, out_shape=(jax.ShapeDtypeStruct((rows, cols), F...  1 us

profile of v4, /device:TPU:0, one launch (start us, length us, event | category | flops | bytes accessed | tf_op | source)
XLA Modules:
  0.0 45.1 jit_solution(11477253528866565517)
XLA Ops:
  0.6 43.4 %shard_map.68 = (f32[128,512]{1,0:T(8,128)S(1)}, f32[3,128,512]{2,1,0:T(8,128)S(1)}) custom-call(f32[16,128,512]{2,1,0:T(8,128)} %ped_h.1, f32[16,128,512]{2,1,0:T(8,128)} %hall_h.1, f32[16,128,512]{2,1,0:T(8,128)} %east_h.1, f32[16,128,512]{2,1,0:T(8,128)} %north_h.1, f32[3,128,512]{2,1,0:T(8,128)} %ion_h.1), custom_call_target="tpu_custom_call" | custom-call | tf_op jit(solution)/shard_map/pallas_call | solution.py:663
  44.1 1.0 %shard_map.69 = (f32[128,512]{1,0:T(8,128)}, f32[3,128,512]{2,1,0:T(8,128)}) custom-call(f32[128,512]{1,0:T(8,128)S(1)} %get-tuple-element.4.pot_v, f32[3,128,512]{2,1,0:T(8,128)S(1)} %get-tuple-element.5.upd_v), custom_call_target="tpu_custom_call" | custom-call | tf_op jit(solution)/shard_map/pallas_call | solution.py:689

commit v5 on v4

--- a/solution.py
+++ b/solution.py
@@ -215,14 +215,12 @@
         rcopy(pk.at[slot], rx.at[0, g], lf, "lon", recv).start()
         rcopy(pk.at[slot + 1], rx.at[1, g], rt, "lon", recv).start()
 
-    columns(0)
-    columns(1)
+    for g in range(4):
+        columns(g)
     pl.semaphore_wait(barrier, n_dev - 1)
     to_up(cur_n.at[:, 8:9], cur_n.at[:, rows + 8 : rows + 9], "n_up")
     to_dn(cur_n.at[:, rows + 7 : rows + 8], cur_n.at[:, 7:8], "n_dn")
-    columns(2)
     send_sig(0, "sig_a")
-    columns(3)
     send_sig(PIECES - 1, "sig_a")
     for q in range(1, PIECES - 1):
         columns(2 * q + 2)
@@ -302,7 +300,6 @@
                 t_out[t, at, :] = d_lon - d_lat
         if q in outer:
             send_t(q, "t_a")
-    send_sig(PIECES - 2, "sig_b")
     mid = (per, n_rt - per)
     edge_in = 128 // (mid[1] - mid[0])
     two_terms(s_one, t_out, rx_in, slot_in, slot_far, [mid], edge_in, "inner")
@@ -411,6 +408,7 @@
     for q in outer:
         combine(sig, sig_rx, S, q)
     lat_send(S, rx_s, GUARD, "s", slot_corner)
+    send_sig(PIECES - 2, "sig_b")
     for i, q in enumerate(outer):
         spread_piece(S, rx_s, slot_s + 2 * i, q, "s_lon")
 

time: 45.2 us -> 45.2 us (level)
  no operation moved by 1% of the time
where the time goes in v5:
time: 45.2 us; the launch traced here: 45 us
  Pallas kernels  44.4 us (98%)
  between operations  0.64 us (1%)
    pallas_call x1, Pallas kernels, shards(): pl.pallas_call(functools.partial(kernel, nlat, nlon, lev, rows, lt), out_...  43.4 us
    pallas_call x1, Pallas kernels, shards(): pl.pallas_call(write_out, out_shape=(jax.ShapeDtypeStruct((rows, cols), F...  1 us

profile of v5, /device:TPU:0, one launch (start us, length us, event | category | flops | bytes accessed | tf_op | source)
XLA Modules:
  0.0 45.0 jit_solution(9636260302067224725)
XLA Ops:
  0.6 43.4 %shard_map.68 = (f32[128,512]{1,0:T(8,128)S(1)}, f32[3,128,512]{2,1,0:T(8,128)S(1)}) custom-call(f32[16,128,512]{2,1,0:T(8,128)} %ped_h.1, f32[16,128,512]{2,1,0:T(8,128)} %hall_h.1, f32[16,128,512]{2,1,0:T(8,128)} %east_h.1, f32[16,128,512]{2,1,0:T(8,128)} %north_h.1, f32[3,128,512]{2,1,0:T(8,128)} %ion_h.1), custom_call_target="tpu_custom_call" | custom-call | tf_op jit(solution)/shard_map/pallas_call | solution.py:661
  44.0 1.0 %shard_map.69 = (f32[128,512]{1,0:T(8,128)}, f32[3,128,512]{2,1,0:T(8,128)}) custom-call(f32[128,512]{1,0:T(8,128)S(1)} %get-tuple-element.4.pot_v, f32[3,128,512]{2,1,0:T(8,128)S(1)} %get-tuple-element.5.upd_v), custom_call_target="tpu_custom_call" | custom-call | tf_op jit(solution)/shard_map/pallas_call | solution.py:687
